TPU v7x, 256 devices: a whole 4x4x8 slice. The times are simulated.
256 devices in a mesh: fsdp: 8 (over x, y_hi), frame: 32 (over y_lo, z, core).
Axes of the slice: x: 4, y: 4 (y_hi: 2, y_lo: 2; y = y_hi * 2 + y_lo), z: 8, core: 2. Of those that a mesh axis runs over, the one named last changes fastest.
Arguments:
- queries: bfloat16 [32, 1024, 1024], P('frame', 'fsdp'), may hold values from -5 to 5
- key_rows: bfloat16 [32, 1024, 1024], P('frame', 'fsdp'), may hold values from -5 to 5
- value_rows: bfloat16 [32, 1024, 1024], P('frame', 'fsdp'), may hold values from -6 to 6
- out_weight: bfloat16 [1024, 2048], P(('fsdp', 'frame')), may hold values from -0.75 to 0.75
- conv_weight: bfloat16 [31, 2048], replicated, may hold values from -1 to 1
- grad_out: bfloat16 [32, 1024, 2048], P('frame', 'fsdp'), may hold values from -6 to 6
Outputs:
- block_out: bfloat16 [32, 1024, 2048], P('frame', 'fsdp')
- grad_queries: bfloat16 [32, 1024, 1024], P('frame', 'fsdp')
- grad_keys: bfloat16 [32, 1024, 1024], P('frame', 'fsdp')
- grad_values: bfloat16 [32, 1024, 1024], P('frame', 'fsdp')
- weight_grad: float32 [1024, 2048], P(('fsdp', 'frame'))
- conv_grad: float32 [31, 2048], replicated
All inputs are finite; a program needn't handle non-finite values.
Results may differ from a plain program's by a relative error of at most 0.014.
Values may be sent and summed in bfloat16 or wider, within the bound.
A program may use at most 128 MiB of HBM per device.

v0:
```python
import math

import jax
import jax.numpy as jnp
from jax import lax
from jax.sharding import PartitionSpec as P

HEADS = 8
HDIM = 128
KERNEL = 31


def with_halo(cells, sides, width):
    for axis, dim in sides:
        count = lax.axis_size(axis)
        ends = count - 1
        head = lax.slice_in_dim(cells, 0, width, axis=dim)
        tail = lax.slice_in_dim(cells, cells.shape[dim] - width, cells.shape[dim], axis=dim)
        cells = jnp.concatenate(
            [
                lax.ppermute(tail, axis, [(i, (i + 1) % count) for i in range(ends)]),
                cells,
                lax.ppermute(head, axis, [((i + 1) % count, i) for i in range(ends)]),
            ],
            axis=dim,
        )
    return cells


def head_scores(queries, key_rows):
    return jnp.einsum("qd,kd->qk", queries, key_rows, preferred_element_type=jnp.float32) * (
        1.0 / math.sqrt(HDIM)
    )


def forward_head(queries, key_rows, value_rows):
    scores = head_scores(queries, key_rows)
    row_max = jnp.max(scores, axis=1)
    exponent = jnp.exp(scores - row_max[:, None])
    row_sum = jnp.sum(exponent, axis=1)
    rounded = (exponent / row_sum[:, None]).astype(jnp.bfloat16)
    attended = jnp.dot(rounded, value_rows, preferred_element_type=jnp.float32).astype(jnp.bfloat16)
    return (attended, row_max, row_sum)


def score_grads(queries, key_rows, value_rows, upstream, row_max, row_sum, row_dot):
    scores = head_scores(queries, key_rows)
    weights = jnp.exp(scores - row_max[:, None]) / row_sum[:, None]
    grad_probs = jnp.einsum("qd,kd->qk", upstream, value_rows, preferred_element_type=jnp.float32)
    if row_dot is None:
        row_dot = jnp.sum(weights * grad_probs, axis=1)
    grad_scores = (weights * (grad_probs - row_dot[:, None])).astype(jnp.bfloat16)
    return (weights, grad_scores, row_dot)


def query_grad(grad_scores, key_rows):
    product = jnp.dot(grad_scores, key_rows, preferred_element_type=jnp.float32)
    return (product * (1.0 / math.sqrt(HDIM))).astype(jnp.bfloat16)


def key_grads(queries, weights, grad_scores, upstream):
    grad_key = jnp.einsum("qk,qd->kd", grad_scores, queries, preferred_element_type=jnp.float32) * (
        1.0 / math.sqrt(HDIM)
    )
    grad_value = jnp.einsum(
        "qk,qd->kd", weights.astype(jnp.bfloat16), upstream, preferred_element_type=jnp.float32
    )
    return (grad_key, grad_value)


def depthwise(signal, taps):
    channels = signal.shape[1]
    result = lax.conv_general_dilated(
        signal[None],
        taps[:, None, :],
        (1,),
        "VALID",
        dimension_numbers=("NWC", "WIO", "NWC"),
        feature_group_count=channels,
        precision=lax.Precision.HIGHEST,
        preferred_element_type=jnp.float32,
    )
    return result[0]


def shards(queries, key_rows, value_rows, out_weight, conv_weight, grad_out):
    local_rows = queries.shape[1]
    half_width = KERNEL // 2
    own_queries = queries[0]
    own_keys = key_rows[0]
    own_values = value_rows[0]
    upstream = grad_out[0].astype(jnp.float32)
    full_weight = lax.all_gather(out_weight, ("fsdp", "frame"), axis=0, tiled=True)
    groups = lax.axis_size("fsdp")
    all_keys, all_values = (
        lax.all_gather(own_keys, "fsdp", axis=0, tiled=True),
        lax.all_gather(own_values, "fsdp", axis=0, tiled=True),
    )
    pieces = []
    maxima = []
    row_sums = []
    for head_index in range(HEADS):
        columns = slice(head_index * HDIM, (head_index + 1) * HDIM)
        attended, row_max, row_sum = forward_head(
            own_queries[:, columns], all_keys[:, columns], all_values[:, columns]
        )
        pieces.append(attended)
        maxima.append(row_max)
        row_sums.append(row_sum)
    attention = jnp.concatenate(pieces, axis=1)
    row_maxes = jnp.stack(maxima, axis=1)
    row_totals = jnp.stack(row_sums, axis=1)
    projected = jnp.dot(attention, full_weight, preferred_element_type=jnp.float32).astype(
        jnp.bfloat16
    )
    padded = with_halo(projected[None], (("fsdp", 1),), half_width)[0].astype(jnp.float32)
    conv_taps = conv_weight.astype(jnp.float32)
    conv_value = depthwise(padded, conv_taps)
    sigmoid_conv = jax.nn.sigmoid(conv_value)
    block_out = (padded[half_width : half_width + local_rows] + conv_value * sigmoid_conv).astype(
        jnp.bfloat16
    )
    grad_conv = (upstream * sigmoid_conv * (1.0 + conv_value * (1.0 - sigmoid_conv))).astype(
        jnp.bfloat16
    )
    grad_padded = with_halo(grad_conv[None], (("fsdp", 1),), half_width)[0].astype(jnp.float32)
    grad_projected = (upstream + depthwise(grad_padded, conv_taps[::-1])).astype(jnp.bfloat16)
    conv_terms = depthwise(padded, grad_conv.astype(jnp.float32))
    total_frames = local_rows * groups * lax.axis_size("frame")
    grad_scale = 1.0 / math.sqrt(total_frames)
    conv_grad = lax.psum(conv_terms, ("fsdp", "frame")) * grad_scale
    weight_grad = (
        lax.psum_scatter(
            jnp.einsum("ri,rd->id", attention, grad_projected, preferred_element_type=jnp.float32),
            ("fsdp", "frame"),
            scatter_dimension=0,
            tiled=True,
        )
        * grad_scale
    )
    grad_attention = jnp.einsum(
        "rd,id->ri", grad_projected, full_weight, preferred_element_type=jnp.float32
    ).astype(jnp.bfloat16)
    query_list = []
    row_dots = []
    for head_index in range(HEADS):
        columns = slice(head_index * HDIM, (head_index + 1) * HDIM)
        weights, grad_scores, row_dot = score_grads(
            own_queries[:, columns],
            all_keys[:, columns],
            all_values[:, columns],
            grad_attention[:, columns],
            row_maxes[:, head_index],
            row_totals[:, head_index],
            None,
        )
        query_list.append(query_grad(grad_scores, all_keys[:, columns]))
        row_dots.append(row_dot)
    row_dot_table = jnp.stack(row_dots, axis=1)
    span_queries, span_grads = (
        lax.all_gather(own_queries, "fsdp", axis=0, tiled=True),
        lax.all_gather(grad_attention, "fsdp", axis=0, tiled=True),
    )
    span_max, span_sum, span_dot = (
        lax.all_gather(row_maxes, "fsdp", axis=0, tiled=True),
        lax.all_gather(row_totals, "fsdp", axis=0, tiled=True),
        lax.all_gather(row_dot_table, "fsdp", axis=0, tiled=True),
    )
    key_list = []
    value_list = []
    for head_index in range(HEADS):
        columns = slice(head_index * HDIM, (head_index + 1) * HDIM)
        weights, grad_scores, unused_dot = score_grads(
            span_queries[:, columns],
            own_keys[:, columns],
            own_values[:, columns],
            span_grads[:, columns],
            span_max[:, head_index],
            span_sum[:, head_index],
            span_dot[:, head_index],
        )
        grad_key, grad_value = key_grads(
            span_queries[:, columns], weights, grad_scores, span_grads[:, columns]
        )
        key_list.append(grad_key.astype(jnp.bfloat16))
        value_list.append(grad_value.astype(jnp.bfloat16))
    grad_queries = jnp.concatenate(query_list, axis=1)
    grad_keys = jnp.concatenate(key_list, axis=1)
    grad_values = jnp.concatenate(value_list, axis=1)
    return (
        block_out[None],
        grad_queries[None],
        grad_keys[None],
        grad_values[None],
        weight_grad,
        conv_grad,
    )


def solution(mesh):
    return jax.shard_map(
        shards,
        mesh=mesh,
        in_specs=(
            P("frame", "fsdp", None),
            P("frame", "fsdp", None),
            P("frame", "fsdp", None),
            P(("fsdp", "frame"), None),
            P(),
            P("frame", "fsdp", None),
        ),
        out_specs=(
            P("frame", "fsdp", None),
            P("frame", "fsdp", None),
            P("frame", "fsdp", None),
            P("frame", "fsdp", None),
            P(("fsdp", "frame"), None),
            P(),
        ),
        check_vma=False,
    )
```

profile of v0, /device:TPU:8, one launch (start us, length us, event | category | flops | bytes accessed | tf_op | source)
XLA Modules:
  0.0 727.6 jit_solution(12551051840050109042)
XLA Ops:
  10.0 7.9 %rev.3 = f32[31,2048]{1,0:T(8,128)} reverse(bf16[31,2048]{1,0:T(8,128)(2,1)} %param.10), dimensions={0} | reverse | bytes 380928 | tf_op jit(solution)/shard_map/rev | solution.py:127
  17.9 54.9 %all-gather.12.cloned.1.call-done = bf16[1,1024,1024]{2,1,0:T(8,128)(2,1)} async-done(((bf16[1,128,1024]{2,1,0:T(8,128)(2,1)}), bf16[1,1024,1024]{2,1,0:T(8,128)(2,1)}) %all-gather.12.cloned.1.call-update) | async-done | bytes 2097168 | tf_op jit(solution)/shard_map/all_gather | solution.py:96
  72.8 1.3 fusion.326
  75.1 1.3 fusion.327
  76.7 1.3 fusion.328
  78.2 1.3 fusion.329
  79.7 1.3 fusion.330
  81.3 1.3 fusion.331
  82.8 1.3 fusion.332
  84.3 1.3 fusion.333
  85.9 34.3 %all_gather.29 = f32[1024,8]{0,1:T(8,128)S(1)} all-gather(f32[128,8]{0,1:T(8,128)S(1)} %stack.7), channel_id=1, replica_groups=mesh['fsdp'=8,'frame'=32] {'fsdp'}, dimensions={0}, use_global_device_ids=true | all-gather | bytes 36864 | tf_op jit(solution)/shard_map/all_gather | solution.py:166
  120.2 34.3 %all_gather.28 = f32[1024,8]{0,1:T(8,128)S(1)} all-gather(f32[128,8]{0,1:T(8,128)S(1)} %stack.6), channel_id=1, replica_groups=mesh['fsdp'=8,'frame'=32] {'fsdp'}, dimensions={0}, use_global_device_ids=true | all-gather | bytes 36864 | tf_op jit(solution)/shard_map/all_gather | solution.py:165
  154.6 1.6 fusion.109
  156.2 1.3 fusion.108
  159.7 36.9 %all-gather.16.cloned.1.call-done = bf16[1,1024,1024]{2,1,0:T(8,128)(2,1)} async-done(((bf16[1,128,1024]{2,1,0:T(8,128)(2,1)}), bf16[1,1024,1024]{2,1,0:T(8,128)(2,1)}) %all-gather.16.cloned.1.call-update) | async-done | bytes 2097168 | tf_op jit(solution)/shard_map/all_gather | solution.py:161
  196.6 2.3 fusion.8
  198.9 1.2 fusion.12
  200.0 1.2 fusion.16
  201.2 1.2 fusion.20
  202.4 1.2 fusion.24
  203.6 1.2 fusion.28
  204.8 1.2 fusion.32
  206.0 109.6 %all-gather.18.cloned.1.call-done = bf16[256,4,2048]{2,1,0:T(4,128)(2,1)} async-done(((bf16[1,4,2048]{2,1,0:T(4,128)(2,1)}), bf16[256,4,2048]{2,1,0:T(4,128)(2,1)}) %all-gather.18.cloned.1.call-update) | async-done | bytes 4194320 | tf_op jit(solution)/shard_map/all_gather | solution.py:93
  315.6 6.9 reshape.105
  322.5 2.9 convolution_convert_fusion
  325.5 1.4 collective-permute-start.1
  326.9 6.1 collective-permute-start
  333.0 2.1 fusion.36
  335.3 8.1 %multiply_convert_fusion = (bf16[1,128,2048]{2,0,1:T(2,128)(2,1)S(1)}, f32[1,128,2048]{2,0,1:T(1,128)S(1)}) fusion(bf16[1,128,2048]{2,1,0:T(8,128)(2,1)S(1)} %copy-done.26, bf16[31,1,2048]{2,0,1:T(8,128)(2,1)S(1)} %bitcast.163, bf16[1,158,2048]{2,1,0:T(8,128)(2,1)S(1)} %pad_maximum_fusion), kind=kOutput, calls=%fused_computation.178 | convolution fusion | flops 18874368 | bytes 2871296 | tf_op jit(solution)/shard_map/conv_general_dilated | solution.py:73
  343.7 1.3 collective-permute-start.3
  345.0 6.3 collective-permute-start.2
  351.3 7.4 %fusion.119 = f32[1,31,2048]{2,0,1:T(1,128)S(1)} fusion(f32[1,128,2048]{2,0,1:T(1,128)S(1)} %get-tuple-element.65, bf16[1,158,2048]{2,1,0:T(8,128)(2,1)S(1)} %pad_maximum_fusion, bf16[1,128,2048]{2,1,0:T(8,128)(2,1)S(1)} %copy-done.26), kind=kOutput, calls=%fused_computation.176 | convolution fusion | flops 18874368 | bytes 2473984 | tf_op jit(solution)/shard_map/conv_general_dilated | solution.py:73
  358.8 1.3 fusion.130
  360.9 4.9 fusion
  366.8 2.3 convolution_convert_fusion.1
  369.1 2.2 multiply_reduce_fusion.7
  371.3 2.0 multiply_reduce_fusion.6
  373.4 1.4 multiply_reduce_fusion.5
  376.6 1.1 multiply_reduce_fusion
  378.2 1.0 fusion.79
  379.2 1.0 fusion.81
  380.3 1.0 fusion.83
  381.3 1.0 fusion.85
  382.3 1.0 fusion.87
  383.3 1.0 fusion.89
  384.3 1.0 fusion.91
  385.3 4.5 fusion.126
  390.8 2.0 fusion.93
  392.8 1.8 copy.25
  394.6 36.9 %all_gather.31 = f32[1024,8]{0,1:T(8,128)S(1)} all-gather(f32[128,8]{0,1:T(8,128)S(1)} %stack.8), channel_id=1, replica_groups=mesh['fsdp'=8,'frame'=32] {'fsdp'}, dimensions={0}, use_global_device_ids=true | all-gather | bytes 36864 | tf_op jit(solution)/shard_map/all_gather | solution.py:167
  431.6 1.5 all-gather.10.cloned.1.call-done
  433.1 2.3 fusion.63
  435.4 2.1 fusion.65
  437.5 2.2 fusion.67
  439.7 2.2 fusion.69
  441.9 2.2 fusion.71
  444.1 2.2 fusion.73
  446.2 2.2 fusion.75
  448.4 2.4 fusion.77
  450.8 1.8 copy.26
  453.2 1.4 fusion.99
  457.1 260.5 %all-reduce.4.cloned.1.call-done = (f32[1024,2048]{1,0:T(8,128)}, f32[31,2048]{1,0:T(8,128)}) async-done(((f32[1024,2048]{1,0:T(8,128)}, f32[31,2048]{1,0:T(8,128)}), (f32[1024,2048]{1,0:T(8,128)}, f32[31,2048]{1,0:T(8,128)})) %all-reduce.4.cloned.1.call-update) | async-done | bytes 8642576
  717.6 1.7 broadcast_multiply_fusion
  719.3 1.5 dynamic-slice_multiply_fusion
  (113 shorter events, 16.4 us)
Async XLA Ops:
  7.2 65.7 %all-gather.12.cloned.1.call-start = ((), (), s32[]{:S(2)}) async-start(), calls=%async_computation.1 | async-start | bytes 2359296 | tf_op jit(solution)/shard_map/all_gather | solution.py:96
  7.9 146.6 %all-gather.14.cloned.1.call-start = ((), (), s32[]{:S(2)}) async-start(), calls=%async_computation.2 | async-start | bytes 2359296 | tf_op jit(solution)/shard_map/all_gather | solution.py:97
  8.6 187.9 %all-gather.16.cloned.1.call-start = ((), (), s32[]{:S(2)}) async-start(), calls=%async_computation.3 | async-start | bytes 2359296 | tf_op jit(solution)/shard_map/all_gather | solution.py:161
  9.4 306.2 %all-gather.18.cloned.1.call-start = ((), (), s32[]{:S(2)}) async-start(), calls=%async_computation.4 | async-start | bytes 4210688 | tf_op jit(solution)/shard_map/all_gather | solution.py:93
  10.0 423.2 %all-gather.10.cloned.1.call-start = ((), (), s32[]{:S(2)}) async-start(), calls=%async_computation | async-start | bytes 2359296 | tf_op jit(solution)/shard_map/all_gather | solution.py:162
  74.1 0.8 copy-start.6
  76.4 4.8 copy-start.2
  154.6 1.6 copy-start.3
  154.6 2.9 copy-start.24
  196.5 2.3 copy-start.20
  196.6 2.3 copy-start.23
  325.4 9.8 %copy-start.22 = (bf16[31,2048]{1,0:T(8,128)(2,1)S(1)}, bf16[31,2048]{1,0:T(8,128)(2,1)}, u32[]{:S(2)}) copy-start(bf16[31,2048]{1,0:T(8,128)(2,1)} %param.10) | copy-start | bytes 380932
  325.4 9.8 %copy-start.26 = (bf16[1,128,2048]{2,1,0:T(8,128)(2,1)S(1)}, bf16[1,128,2048]{2,1,0:T(8,128)(2,1)}, u32[]{:S(2)}) copy-start(bf16[1,128,2048]{2,1,0:T(8,128)(2,1)} %param.11) | copy-start | bytes 1572868
  325.5 9.6 %collective-permute-start.1 = (bf16[1,15,2048]{2,1,0:T(8,128)(2,1)S(1)}, bf16[1,15,2048]{2,1,0:T(8,128)(2,1)S(1)}, u32[]{:S(2)}, u32[]{:S(2)}) collective-permute-start(bf16[1,15,2048]{2,1,0:T(8,128)(2,1)S(1)} %get-tuple-element.23), channel_id=1, source_target_pairs={{32,0},{64,32},{96,64},{128,96},{160,128},{192,160},{224,192},{33,... | collective-permute-start | bytes 184328 | tf_op jit(solution)/shard_map/ppermute | solution.py:23
  326.9 8.2 %collective-permute-start = (bf16[1,15,2048]{2,1,0:T(8,128)(2,1)S(1)}, bf16[1,15,2048]{2,1,0:T(8,128)(2,1)S(1)}, u32[]{:S(2)}, u32[]{:S(2)}) collective-permute-start(bf16[1,15,2048]{2,1,0:T(8,128)(2,1)S(1)} %get-tuple-element.22), channel_id=1, source_target_pairs={{0,32},{32,64},{64,96},{96,128},{128,160},{160,192},{192,224},{1,3... | collective-permute-start | bytes 184328 | tf_op jit(solution)/shard_map/ppermute | solution.py:21
  343.7 17.2 %collective-permute-start.3 = (bf16[1,15,2048]{2,0,1:T(2,128)(2,1)S(1)}, bf16[1,15,2048]{2,0,1:T(2,128)(2,1)S(1)}, u32[]{:S(2)}, u32[]{:S(2)}) collective-permute-start(bf16[1,15,2048]{2,0,1:T(2,128)(2,1)S(1)} %get-tuple-element.21), channel_id=1, source_target_pairs={{32,0},{64,32},{96,64},{128,96},{160,128},{192,160},{224,192},{33,... | collective-permute-start | bytes 184328 | tf_op jit(solution)/shard_map/ppermute | solution.py:23
  345.0 15.9 %collective-permute-start.2 = (bf16[1,15,2048]{2,0,1:T(2,128)(2,1)S(1)}, bf16[1,15,2048]{2,0,1:T(2,128)(2,1)S(1)}, u32[]{:S(2)}, u32[]{:S(2)}) collective-permute-start(bf16[1,15,2048]{2,0,1:T(2,128)(2,1)S(1)} %get-tuple-element.20), channel_id=1, source_target_pairs={{0,32},{32,64},{64,96},{96,128},{128,160},{160,192},{192,224},{1,3... | collective-permute-start | bytes 184328 | tf_op jit(solution)/shard_map/ppermute | solution.py:21
  358.7 2.2 copy-start.19
  360.9 5.9 copy-start
  365.9 1.0 copy-start.9
  369.1 2.2 copy-start.4
  373.4 344.2 %all-reduce.4.cloned.1.call-start = ((), (), s32[]{:S(2)}) async-start(), calls=%async_computation.5 | async-start | bytes 17301504
  373.4 1.5 copy-start.11
  373.4 1.8 copy-start.25
  376.2 1.5 copy-start.7
  376.2 2.0 copy-start.8
  376.2 2.0 copy-start.29
  376.6 2.7 copy-start.5
  376.6 2.7 copy-start.28
  383.3 2.0 copy-start.10
  389.8 1.0 copy-start.27
  389.8 43.3 %copy-start.12 = (f32[1024,128]{1,0:T(8,128)S(1)}, f32[1024,128]{1,0:T(8,128)}, u32[]{:S(2)}) copy-start(f32[1024,128]{1,0:T(8,128)} %fusion.8) | copy-start | bytes 1572868
  389.8 43.3 %copy-start.21 = (bf16[1,128,1024]{2,1,0:T(8,128)(2,1)S(1)}, bf16[1,128,1024]{2,1,0:T(8,128)(2,1)}, u32[]{:S(2)}) copy-start(bf16[1,128,1024]{2,1,0:T(8,128)(2,1)} %param.8) | copy-start | bytes 786436
  390.8 44.6 %copy-start.13 = (f32[1024,128]{1,0:T(8,128)S(1)}, f32[1024,128]{1,0:T(8,128)}, u32[]{:S(2)}) copy-start(f32[1024,128]{1,0:T(8,128)} %fusion.12) | copy-start | bytes 1572868
  433.1 4.4 copy-start.1
  452.6 2.0 copy-start.14
  452.6 2.3 copy-start.15
  452.6 2.7 copy-start.16
  452.9 2.7 copy-start.17
  453.2 2.7 copy-start.18
Sparse Core Ops, SparseCore 0:
  10.6 62.1 all-gather.11
  75.5 59.2 all-gather.13
  137.4 59.0 all-gather.15
  200.1 115.4 all-gather.17
  373.5 59.6 all-gather.9
  438.7 278.8 all-reduce.3
where the time goes:
time: 729 us; the launch traced here: 728 us
  waiting for transfers between devices  466 us (64%)
  blocking collectives  105 us (14%)
  matrix products  95.3 us (13%)
  local copies, waits for them, and re-layouts  24.2 us (3%)
  starting transfers between devices  15.3 us (2%)
  between operations  14.6 us (2%)
    unnamed x7, waiting for transfers between devices  263 us
    all_gather x1, waiting for transfers between devices, shards(): lax.all_gather(out_weight, ('fsdp', 'frame'), axis=0, tiled=True)  110 us
    all_gather x1, waiting for transfers between devices, shards(): lax.all_gather(own_keys, 'fsdp', axis=0, tiled=True)  54.9 us
    all_gather x1, blocking collectives, shards(): lax.all_gather(row_dot_table, 'fsdp', axis=0, tiled=True)  36.9 us
    all_gather x1, waiting for transfers between devices, shards(): lax.all_gather(own_queries, 'fsdp', axis=0, tiled=True)  36.9 us
    all_gather x1, blocking collectives, shards(): lax.all_gather(row_totals, 'fsdp', axis=0, tiled=True)  34.3 us
    all_gather x1, blocking collectives, shards(): lax.all_gather(row_maxes, 'fsdp', axis=0, tiled=True)  34.3 us
    dot_general x16, matrix products, head_scores(): jnp.einsum('qd,kd->qk', queries, key_rows, preferred_element_type=jnp.flo...  21.8 us
  transfers between devices with their start and end apart: 10, of which 5 were waited for; matrix products, arithmetic and copies ran while one was open for 12% of the time, Pallas kernels for 0%

commit v1 on v0

v1 whole, which is shorter than its diff:
```python
import math

import jax
import jax.numpy as jnp
from jax import lax
from jax.experimental import pallas as pl
from jax.experimental.pallas import tpu as pltpu
from jax.sharding import PartitionSpec as P

MESH = pl.DeviceIdType.MESH
HDIM = 128
KERNEL = 31
ROWS = 128
INNER = 1024
D = 2048
SPAN = 1024
FS = 8
NZ = 8
NP = 16
HALO = 32
COLS = 256
BLK = 256
INV_ROOT = 1.0 / math.sqrt(HDIM)
EXP_SCALE = INV_ROOT * math.log2(math.e)
F32 = jnp.float32
BF16 = jnp.bfloat16


def mod(a, n):
    return lax.rem(a, jnp.int32(n))


def remote(src, dst, send, recv, device):
    return pltpu.make_async_remote_copy(
        src_ref=src, dst_ref=dst, send_sem=send, recv_sem=recv, device_id=device, device_id_type=MESH
    )


def loop(lower, upper, body):
    def step(i, carry):
        body(i)
        return carry

    lax.fori_loop(lower, upper, step, 0)


def at128(i):
    return pl.ds(pl.multiple_of(i * 128, 128), 128)


def at64(i):
    return pl.ds(pl.multiple_of(i * 64, 64), 64)


def dot_nt(a, b):
    return lax.dot_general(a, b, (((1,), (1,)), ((), ())), preferred_element_type=F32)


def dot_tn(a, b):
    return lax.dot_general(a, b, (((0,), (0,)), ((), ())), preferred_element_type=F32)


def kernel(
    q_ref, k_ref, v_ref, w_ref, taps_ref, go_ref,
    o_block, o_gq, o_gk, o_gv, o_wg, o_cg,
    qkvh, prob, ohp, attx, wpl, wtmp, wbuf, perm, attp, attt, gox, tapf, proj_s, gc_s, wgs,
    ga_acc, ga_s, gh, dh, dk_acc, dv_acc, pbuf, sbuf, rbuf, wgp_s, wgp_r,
    tapg, ta, tp_s, tp_r, tb, tc_s, tc,
    qkv_ss, qkv_rs, wpl_ss, wpl_rs, go_ss, go_rs, ag_ss, ag_rs, agp_ss, agp_rs, att_ss, att_rs,
    ga_ss, ga_rs, rsp_ss, rsp_rs, rs_ss, rs_rs, d_ss, d_rs, wgp_ss, wgp_rs,
    ta_ss, ta_rs, tp_ss, tp_rs, tb_ss, tb_rs, tc_ss, tc_rs,
):
    f = lax.axis_index("fsdp").astype(jnp.int32)
    r = lax.axis_index("frame").astype(jnp.int32)
    ylo = lax.div(r, jnp.int32(16))
    z = mod(lax.div(r, jnp.int32(2)), NZ)
    core = mod(r, 2)
    me = f * 2 + ylo

    def plane(p):
        return (lax.div(p, jnp.int32(2)), mod(p, 2) * 16 + z * 2 + core)

    def zline(other):
        return (f, ylo * 16 + other * 2 + core)

    partner = (f, ylo * 16 + z * 2 + 1 - core)

    barrier = pltpu.get_barrier_semaphore()

    def greet_plane(k):
        pl.semaphore_signal(barrier, inc=1, device_id=plane(mod(me + k, NP)), device_id_type=MESH)

    def greet_z(k):
        pl.semaphore_signal(barrier, inc=1, device_id=zline(mod(z + k, NZ)), device_id_type=MESH)

    loop(1, NP, greet_plane)
    loop(1, NZ, greet_z)
    pl.semaphore_signal(barrier, inc=1, device_id=partner, device_id_type=MESH)
    pl.semaphore_wait(barrier, NP - 1 + NZ - 1 + 1)

    def wpl_copy(k):
        return remote(w_ref, wpl.at[me], wpl_ss.at[k], wpl_rs.at[k], plane(mod(me + k, NP)))

    loop(1, NP, lambda k: wpl_copy(k).start())

    heads = ((q_ref, 0), (k_ref, 1), (v_ref, 2))

    def qkv_copy(k, source, slot):
        peer = mod(f + k, FS)
        return remote(
            source.at[:, at128(peer)], qkvh.at[slot, at128(f), :], qkv_ss.at[slot, k], qkv_rs.at[slot, k], (peer, r)
        )

    def qkv_start(k):
        for source, slot in heads:
            qkv_copy(k, source, slot).start()

    loop(1, FS, qkv_start)

    def go_down():
        return remote(go_ref.at[pl.ds(0, 16), :], gox.at[pl.ds(144, 16), :], go_ss.at[0], go_rs.at[0], (f - 1, r))

    def go_up():
        return remote(go_ref.at[pl.ds(112, 16), :], gox.at[pl.ds(0, 16), :], go_ss.at[1], go_rs.at[1], (f + 1, r))

    @pl.when(f > 0)
    def _():
        go_down().start()

    @pl.when(f < FS - 1)
    def _():
        go_up().start()

    for source, slot in heads:
        qkvh[slot, at128(f), :] = source[:, at128(f)]
    gox[16:144, :] = go_ref[...]

    @pl.when(f == 0)
    def _():
        gox[0:16, :] = jnp.zeros((16, D), BF16)

    @pl.when(f == FS - 1)
    def _():
        gox[144:160, :] = jnp.zeros((16, D), BF16)

    ohp[0:HALO, :] = jnp.zeros((HALO, HDIM), BF16)
    ohp[HALO + SPAN : HALO + SPAN + HALO, :] = jnp.zeros((HALO, HDIM), BF16)
    tapf[0:KERNEL, :] = taps_ref[...].astype(F32)
    wpl[me] = w_ref[...]

    def perm_rows(b):
        row = lax.broadcasted_iota(jnp.int32, (128, INNER), 0) + b * 128
        col = lax.broadcasted_iota(jnp.int32, (128, INNER), 1)
        at = ((col >> 2) & 15) * 64 + ((col >> 6) & 7) * 8 + (col >> 9) * 4 + (col & 3)
        perm[at128(b), :] = jnp.where(row == at, 1.0, 0.0).astype(BF16)

    loop(0, 8, perm_rows)

    def wpl_arrived(k):
        source = mod(me - k + NP, NP)
        remote(w_ref, wpl.at[source], wpl_ss.at[k], wpl_rs.at[k], plane(source)).wait_recv()

    loop(1, NP, wpl_arrived)
    for p in range(NP):
        wtmp[4 * p : 4 * p + 4, :] = wpl[p].astype(F32)

    def wblock(c, zz):
        return pl.ds(pl.multiple_of(c * 512 + zz * 64, 64), 64)

    wbuf[wblock(core, z), :] = wtmp[...].astype(BF16)

    up, down = zline(mod(z + 1, NZ)), zline(mod(z + NZ - 1, NZ))

    def ag_copy(way, s, part):
        block = mod(z - s + NZ, NZ) if way == 0 else mod(z + s, NZ)
        view = wbuf.at[wblock(core, block), pl.ds(part * 1024, 1024)]
        return remote(view, view, ag_ss.at[way, s, part], ag_rs.at[way, s, part], up if way == 0 else down)

    def ag_arrived(way, s, part):
        block = mod(z - 1 - s + NZ, NZ) if way == 0 else mod(z + 1 + s, NZ)
        view = wbuf.at[wblock(core, block), pl.ds(part * 1024, 1024)]
        remote(view, view, ag_ss.at[way, s, part], ag_rs.at[way, s, part], down if way == 0 else up).wait_recv()

    def agp_copy(k):
        view = wbuf.at[wblock(core, mod(z + k, NZ)), :]
        return remote(view, view, agp_ss.at[k], agp_rs.at[k], partner)

    def agp_arrived(k):
        view = wbuf.at[wblock(1 - core, mod(z + k, NZ)), :]
        remote(view, view, agp_ss.at[k], agp_rs.at[k], partner).wait_recv()

    for part in range(2):
        for way in range(2):
            ag_copy(way, 0, part).start()
    agp_copy(0).start()

    def ag_turn(s):
        for part in range(2):
            for way in range(2):
                ag_arrived(way, s, part)
                if s + 1 < 3 or part == way:
                    ag_copy(way, s + 1, part).start()
        agp_copy(NZ - 1 - s).start()
        agp_copy(1 + s).start()

    ag_turn(0)

    def qkv_arrived(k):
        source = mod(f - k + FS, FS)
        for ref, slot in heads:
            remote(
                ref.at[:, at128(source)], qkvh.at[slot, at128(source), :], qkv_ss.at[slot, k], qkv_rs.at[slot, k], (source, r)
            ).wait_recv()

    loop(1, FS, qkv_arrived)

    def attend(i):
        rows = pl.ds(pl.multiple_of(i * BLK, BLK), BLK)
        scores = dot_nt(qkvh[0, rows, :], qkvh[1])
        exponent = jnp.exp2((scores - jnp.max(scores, axis=1, keepdims=True)) * EXP_SCALE)
        rounded = (exponent * (1.0 / jnp.sum(exponent, axis=1, keepdims=True))).astype(BF16)
        prob[rows, :] = rounded
        attended = jnp.dot(rounded, qkvh[2], preferred_element_type=F32)
        ohp[pl.ds(pl.multiple_of(i * BLK + HALO, HALO), BLK), :] = attended.astype(BF16)

    loop(0, 2, attend)
    ag_turn(1)
    loop(2, 4, attend)

    def ext(i):
        return pl.ds(pl.multiple_of(i * ROWS, ROWS), ROWS + 2 * HALO)

    def att_copy(k):
        peer = mod(f + k, FS)
        return remote(ohp.at[ext(peer), :], attx.at[:, at128(f)], att_ss.at[k], att_rs.at[k], (peer, r))

    def att_arrived(k):
        source = mod(f - k + FS, FS)
        remote(ohp.at[ext(source), :], attx.at[:, at128(source)], att_ss.at[k], att_rs.at[k], (source, r)).wait_recv()

    loop(1, FS, lambda k: att_copy(k).start())
    attx[:, at128(f)] = ohp[ext(f), :]
    ag_turn(2)
    ag_arrived(0, 3, 0)
    ag_arrived(1, 3, 1)
    agp_copy(4).start()

    @pl.when(f < FS - 1)
    def _():
        remote(go_ref.at[pl.ds(0, 16), :], gox.at[pl.ds(144, 16), :], go_ss.at[0], go_rs.at[0], (f + 1, r)).wait_recv()

    @pl.when(f > 0)
    def _():
        remote(go_ref.at[pl.ds(112, 16), :], gox.at[pl.ds(0, 16), :], go_ss.at[1], go_rs.at[1], (f - 1, r)).wait_recv()

    loop(1, FS, att_arrived)
    attp[...] = jnp.dot(attx[...], perm[...], preferred_element_type=F32).astype(BF16)
    attt[...] = attp[HALO : HALO + ROWS, :].T
    loop(0, NZ, agp_arrived)
    ga_acc[...] = jnp.zeros((ROWS, INNER), F32)
    tapg[KERNEL : KERNEL + 1, :] = jnp.zeros((1, D), F32)

    def columns(c):
        cols = pl.ds(pl.multiple_of(c * COLS, COLS), COLS)
        weight = wbuf[:, cols]
        proj_s[...] = jnp.dot(attp[...], weight, preferred_element_type=F32).astype(BF16).astype(F32)
        for lane in range(COLS // 128):
            here = pl.ds(pl.multiple_of(c * COLS + lane * 128, 128), 128)
            local = slice(lane * 128, lane * 128 + 128)
            conv = jnp.zeros((160, 128), F32)
            for j in range(KERNEL):
                conv = conv + tapf[j : j + 1, here] * proj_s[1 + j : 161 + j, local]
            sig = jax.nn.sigmoid(conv)
            upstream = gox[:, here].astype(F32)
            o_block[:, here] = (proj_s[32:160, local] + conv[16:144] * sig[16:144]).astype(BF16)
            gc_s[:, local] = (upstream * sig * (1.0 + conv * (1.0 - sig))).astype(BF16).astype(F32)
            total = go_ref[:, here].astype(F32)
            for j in range(KERNEL):
                total = total + tapf[j : j + 1, here] * gc_s[31 - j : 159 - j, local]
            gp = total.astype(BF16)
            gc_own = gc_s[16:144, local]
            for j in range(KERNEL):
                tapg[j : j + 1, here] = jnp.sum(gc_own * proj_s[17 + j : 145 + j, local], axis=0, keepdims=True)
            wgs[:, here] = jnp.dot(attt[...], gp, preferred_element_type=F32).astype(BF16)
            ga_acc[...] += dot_nt(gp, wbuf[:, here])

    loop(0, D // COLS, columns)
    ga_s[...] = dot_nt(ga_acc[...].astype(BF16), perm[...]).astype(BF16)

    def ga_copy(k):
        peer = mod(f + k, FS)
        return remote(ga_s.at[:, at128(peer)], gh.at[at128(f), :], ga_ss.at[k], ga_rs.at[k], (peer, r))

    def ga_arrived(k):
        source = mod(f - k + FS, FS)
        remote(ga_s.at[:, at128(source)], gh.at[at128(source), :], ga_ss.at[k], ga_rs.at[k], (source, r)).wait_recv()

    loop(1, FS, lambda k: ga_copy(k).start())

    def rsp_copy(k):
        block = mod(z + k, NZ)
        return remote(wgs.at[wblock(1 - core, block), :], pbuf.at[at64(block), :], rsp_ss.at[k], rsp_rs.at[k], partner)

    def rsp_arrived(k):
        block = mod(z + k, NZ)
        remote(wgs.at[wblock(core, block), :], pbuf.at[at64(block), :], rsp_ss.at[k], rsp_rs.at[k], partner).wait_recv()

    for k in (7, 1, 6, 2, 5, 3, 4, 0):
        rsp_copy(k).start()

    def ta_copy(k):
        peer = mod(me + k, NP)
        return remote(tapg.at[:, at128(peer)], ta.at[k], ta_ss.at[k], ta_rs.at[k], plane(peer))

    def ta_arrived(k):
        source = mod(me - k + NP, NP)
        remote(tapg.at[:, at128(source)], ta.at[k], ta_ss.at[k], ta_rs.at[k], plane(source)).wait_recv()

    loop(1, NP, lambda k: ta_copy(k).start())
    gh[at128(f), :] = ga_s[:, at128(f)]

    def rs_copy(way, s, part):
        piece = pl.ds(part * 512, 512)
        return remote(
            sbuf.at[s, way, :, piece], rbuf.at[s, way, :, piece], rs_ss.at[s, way, part], rs_rs.at[s, way, part],
            up if way == 0 else down,
        )

    def rs_arrived(way, s, part):
        piece = pl.ds(part * 512, 512)
        remote(
            sbuf.at[s, way, :, piece], rbuf.at[s, way, :, piece], rs_ss.at[s, way, part], rs_rs.at[s, way, part],
            down if way == 0 else up,
        ).wait_recv()

    def chip_sum(block, cols):
        return wgs[wblock(core, block), cols].astype(F32) + pbuf[at64(block), cols].astype(F32)

    def rs_turn(s):
        if s < 4:
            rsp_arrived(NZ - 1 - s)
        if s < 3:
            rsp_arrived(1 + s)
        for part in range(2):
            for way in range(2):
                block = mod(z - 1 - s + NZ, NZ) if way == 0 else mod(z + 1 + s, NZ)
                piece = slice(part * 512, part * 512 + 512)
                value = chip_sum(block, slice(way * 1024 + part * 512, way * 1024 + part * 512 + 512))
                if s > 0:
                    rs_arrived(way, s - 1, part)
                    value = value + rbuf[s - 1, way, :, piece].astype(F32)
                sbuf[s, way, :, piece] = value.astype(BF16)
                rs_copy(way, s, part).start()

    rs_turn(0)
    loop(1, FS, ga_arrived)
    dk_acc[...] = jnp.zeros((SPAN, HDIM), F32)
    dv_acc[...] = jnp.zeros((SPAN, HDIM), F32)

    def attend_back(i):
        rows = pl.ds(pl.multiple_of(i * BLK, BLK), BLK)
        grad = gh[rows, :]
        rounded = prob[rows, :]
        weights = rounded.astype(F32)
        grad_probs = dot_nt(grad, qkvh[2])
        row_dot = jnp.sum(weights * grad_probs, axis=1, keepdims=True)
        grad_scores = (weights * (grad_probs - row_dot)).astype(BF16)
        dh[0, rows, :] = (jnp.dot(grad_scores, qkvh[1], preferred_element_type=F32) * INV_ROOT).astype(BF16)
        dk_acc[...] += dot_tn(grad_scores, qkvh[0, rows, :])
        dv_acc[...] += dot_tn(rounded, grad)

    def tp_copy():
        return remote(tp_s, tp_r, tp_ss, tp_rs, partner)

    def tb_copy(k):
        return remote(tb.at[z], tb.at[z], tb_ss.at[k], tb_rs.at[k], zline(mod(z + k, NZ)))

    def tb_arrived(k):
        source = mod(z - k + NZ, NZ)
        remote(tb.at[source], tb.at[source], tb_ss.at[k], tb_rs.at[k], zline(source)).wait_recv()

    def tc_copy(k):
        return remote(tc_s, tc.at[me], tc_ss.at[k], tc_rs.at[k], plane(mod(me + k, NP)))

    def tc_arrived(k):
        source = mod(me - k + NP, NP)
        remote(tc_s, tc.at[source], tc_ss.at[k], tc_rs.at[k], plane(source)).wait_recv()

    loop(0, 1, attend_back)
    loop(1, NP, ta_arrived)
    total = tapg[:, at128(me)]
    for k in range(1, NP):
        total = total + ta[k]
    tp_s[...] = total
    tp_copy().start()
    rs_turn(1)
    loop(1, 2, attend_back)
    tp_copy().wait_recv()
    tb[z] = tp_s[...] + tp_r[...]
    loop(1, NZ, lambda k: tb_copy(k).start())
    rs_turn(2)
    loop(2, 4, attend_back)
    dh[1] = (dk_acc[...] * INV_ROOT).astype(BF16)
    dh[2] = dv_acc[...].astype(BF16)

    outs = ((o_gq, 0), (o_gk, 1), (o_gv, 2))

    def d_copy(k, ref, slot):
        peer = mod(f + k, FS)
        return remote(dh.at[slot, at128(peer), :], ref.at[:, at128(f)], d_ss.at[slot, k], d_rs.at[slot, k], (peer, r))

    def d_start(k):
        for ref, slot in outs:
            d_copy(k, ref, slot).start()

    def d_arrived(k):
        source = mod(f - k + FS, FS)
        for ref, slot in outs:
            remote(
                dh.at[slot, at128(source), :], ref.at[:, at128(source)], d_ss.at[slot, k], d_rs.at[slot, k], (source, r)
            ).wait_recv()

    loop(1, FS, d_start)
    for ref, slot in outs:
        ref[:, at128(f)] = dh[slot, at128(f), :]
    rs_turn(3)
    loop(1, NZ, tb_arrived)
    total = tb[0]
    for k in range(1, NZ):
        total = total + tb[k]
    grad_scale = 1.0 / math.sqrt(SPAN * 32)
    tc_s[...] = total * grad_scale
    loop(1, NP, lambda k: tc_copy(k).start())
    tc[me] = tc_s[...]
    rs_turn(4)
    rs_turn(5)
    rs_turn(6)
    rsp_arrived(0)
    for part in range(2):
        for way in range(2):
            cols = slice(way * 1024 + part * 512, way * 1024 + part * 512 + 512)
            rs_arrived(way, 6, part)
            wtmp[:, cols] = chip_sum(z, cols) + rbuf[6, way, :, part * 512 : part * 512 + 512].astype(F32)
    for p in range(NP):
        wgp_s[p] = wtmp[4 * p : 4 * p + 4, :]

    def wgp_copy(k):
        peer = mod(me + k, NP)
        return remote(wgp_s.at[peer], wgp_r.at[k], wgp_ss.at[k], wgp_rs.at[k], plane(peer))

    def wgp_arrived(k):
        source = mod(me - k + NP, NP)
        remote(wgp_s.at[source], wgp_r.at[k], wgp_ss.at[k], wgp_rs.at[k], plane(source)).wait_recv()

    loop(1, NP, lambda k: wgp_copy(k).start())
    loop(1, NP, tc_arrived)
    for p in range(NP):
        o_cg[:, p * 128 : p * 128 + 128] = tc[p, 0:KERNEL, :]
    loop(1, FS, d_arrived)
    loop(1, NP, wgp_arrived)
    total = wgp_s[me]
    for k in range(1, NP):
        total = total + wgp_r[k]
    o_wg[...] = total * grad_scale

    def plane_sent(k):
        wpl_copy(k).wait_send()
        ta_copy(k).wait_send()
        tc_copy(k).wait_send()
        wgp_copy(k).wait_send()

    def span_sent(k):
        for ref, slot in heads:
            qkv_copy(k, ref, slot).wait_send()
        for ref, slot in outs:
            d_copy(k, ref, slot).wait_send()
        att_copy(k).wait_send()
        ga_copy(k).wait_send()

    loop(1, NP, plane_sent)
    loop(1, FS, span_sent)

    @pl.when(f > 0)
    def _():
        go_down().wait_send()

    @pl.when(f < FS - 1)
    def _():
        go_up().wait_send()

    for way in range(2):
        for part in range(2):
            for s in range(4):
                if s < 3 or part == way:
                    ag_copy(way, s, part).wait_send()
            for s in range(7):
                rs_copy(way, s, part).wait_send()

    def line_sent(k):
        agp_copy(k).wait_send()
        rsp_copy(k).wait_send()

    loop(0, NZ, line_sent)
    loop(1, NZ, lambda k: tb_copy(k).wait_send())
    tp_copy().wait_send()


def shards(queries, key_rows, value_rows, out_weight, conv_weight, grad_out):
    vmem = pl.BlockSpec(memory_space=pltpu.VMEM)
    dma = pltpu.SemaphoreType.DMA
    block_out, grad_queries, grad_keys, grad_values, weight_grad, conv_grad = pl.pallas_call(
        kernel,
        out_shape=(
            jax.ShapeDtypeStruct((ROWS, D), BF16),
            jax.ShapeDtypeStruct((ROWS, INNER), BF16),
            jax.ShapeDtypeStruct((ROWS, INNER), BF16),
            jax.ShapeDtypeStruct((ROWS, INNER), BF16),
            jax.ShapeDtypeStruct((4, D), F32),
            jax.ShapeDtypeStruct((KERNEL, D), F32),
        ),
        in_specs=[vmem] * 6,
        out_specs=(vmem,) * 6,
        scratch_shapes=[
            pltpu.VMEM((3, SPAN, HDIM), BF16),
            pltpu.VMEM((SPAN, SPAN), BF16),
            pltpu.VMEM((SPAN + 2 * HALO, HDIM), BF16),
            pltpu.VMEM((ROWS + 2 * HALO, INNER), BF16),
            pltpu.VMEM((NP, 4, D), BF16),
            pltpu.VMEM((64, D), F32),
            pltpu.VMEM((INNER, D), BF16),
            pltpu.VMEM((INNER, INNER), BF16),
            pltpu.VMEM((ROWS + 2 * HALO, INNER), BF16),
            pltpu.VMEM((INNER, ROWS), BF16),
            pltpu.VMEM((160, D), BF16),
            pltpu.VMEM((32, D), F32),
            pltpu.VMEM((ROWS + 2 * HALO, COLS), F32),
            pltpu.VMEM((160, COLS), F32),
            pltpu.VMEM((INNER, D), BF16),
            pltpu.VMEM((ROWS, INNER), F32),
            pltpu.VMEM((ROWS, INNER), BF16),
            pltpu.VMEM((SPAN, HDIM), BF16),
            pltpu.VMEM((3, SPAN, HDIM), BF16),
            pltpu.VMEM((SPAN, HDIM), F32),
            pltpu.VMEM((SPAN, HDIM), F32),
            pltpu.VMEM((512, D), BF16),
            pltpu.VMEM((7, 2, 64, 1024), BF16),
            pltpu.VMEM((7, 2, 64, 1024), BF16),
            pltpu.VMEM((NP, 4, D), F32),
            pltpu.VMEM((NP, 4, D), F32),
            pltpu.VMEM((32, D), F32),
            pltpu.VMEM((NP, 32, 128), F32),
            pltpu.VMEM((32, 128), F32),
            pltpu.VMEM((32, 128), F32),
            pltpu.VMEM((NZ, 32, 128), F32),
            pltpu.VMEM((32, 128), F32),
            pltpu.VMEM((NP, 32, 128), F32),
            dma((3, FS)), dma((3, FS)),
            dma((NP,)), dma((NP,)),
            dma((2,)), dma((2,)),
            dma((2, 4, 2)), dma((2, 4, 2)),
            dma((NZ,)), dma((NZ,)),
            dma((FS,)), dma((FS,)),
            dma((FS,)), dma((FS,)),
            dma((NZ,)), dma((NZ,)),
            dma((7, 2, 2)), dma((7, 2, 2)),
            dma((3, FS)), dma((3, FS)),
            dma((NP,)), dma((NP,)),
            dma((NP,)), dma((NP,)),
            dma, dma,
            dma((NZ,)), dma((NZ,)),
            dma((NP,)), dma((NP,)),
        ],
        compiler_params=pltpu.CompilerParams(
            collective_id=0, has_side_effects=True, vmem_limit_bytes=60 * 1024 * 1024
        ),
    )(queries[0], key_rows[0], value_rows[0], out_weight, conv_weight, grad_out[0])
    return (block_out[None], grad_queries[None], grad_keys[None], grad_values[None], weight_grad, conv_grad)


def solution(mesh):
    return jax.shard_map(
        shards,
        mesh=mesh,
        in_specs=(
            P("frame", "fsdp", None),
            P("frame", "fsdp", None),
            P("frame", "fsdp", None),
            P(("fsdp", "frame"), None),
            P(),
            P("frame", "fsdp", None),
        ),
        out_specs=(
            P("frame", "fsdp", None),
            P("frame", "fsdp", None),
            P("frame", "fsdp", None),
            P("frame", "fsdp", None),
            P(("fsdp", "frame"), None),
            P(),
        ),
        check_vma=False,
    )
```

time: 729 us -> 124 us (0.17)
  waiting for transfers between devices: 466 us -> 0 us
  Pallas kernels: 0 us -> 117 us
  blocking collectives: 105 us -> 0 us
  matrix products: 95.3 us -> 0 us
  local copies, waits for them, and re-layouts: 24.2 us -> 6.09 us
  starting transfers between devices: 15.3 us -> 0 us
  between operations: 14.6 us -> 0.66 us
    unnamed x7 -> x0, waiting for transfers between devices: 263 us -> none
    all_gather x5 -> x0, waiting for transfers between devices: 203 us -> none  [the longest x1 110 us: shards(): lax.all_gather(out_weight, ('fsdp', 'frame'), axis=0, tiled=True)]
    pallas_call x0 -> x1, Pallas kernels: none -> 117 us  [shards(): pl.pallas_call(kernel, out_shape=(jax.ShapeDtypeStruct((ROWS, D), BF16),...]
    all_gather x3 -> x0, blocking collectives: 105 us -> none  [the longest x1 36.9 us: shards(): lax.all_gather(row_dot_table, 'fsdp', axis=0, tiled=True)]
    dot_general x59 -> x0, matrix products: 74.9 us -> none  [the longest x16 21.8 us: head_scores(): jnp.einsum('qd,kd->qk', queries, key_rows, preferred_element_type=jnp.flo...]
    conv_general_dilated x3 -> x0, matrix products: 20.4 us -> none  [depthwise(): lax.conv_general_dilated(signal[None], taps[:, None, :], (1,), 'VALID', d...]
    ppermute x4 -> x0, starting transfers between devices: 15.1 us -> none  [the longest x2 12.4 us: with_halo(): lax.ppermute(tail, axis, [(i, (i + 1) % count) for i in range(ends)])]
    unnamed x65 -> x16, local copies, waits for them, and re-layouts: 15.9 us -> 6.09 us
  transfers between devices with their start and end apart: 10 -> 0, of which waited for: 5 -> 0; matrix products, arithmetic and copies ran while one was open for 12% -> 0% of each run, Pallas kernels for 0% -> 0%
where the time goes in v1:
time: 124 us
  Pallas kernels  117 us (94%)
  local copies, waits for them, and re-layouts  6.09 us (5%)
    pallas_call x1, Pallas kernels, shards(): pl.pallas_call(kernel, out_shape=(jax.ShapeDtypeStruct((ROWS, D), BF16),...  117 us
    unnamed x16, local copies, waits for them, and re-layouts  6.09 us

profile of v1, /device:TPU:8, one launch (start us, length us, event | category | flops | bytes accessed | tf_op | source)
XLA Modules:
  0.0 123.6 jit_solution(8478609035768613392)
XLA Ops:
  0.6 116.9 %shard_map.109 = (bf16[128,2048]{1,0:T(8,128)(2,1)}, bf16[128,1024]{1,0:T(8,128)(2,1)}, bf16[128,1024]{1,0:T(8,128)(2,1)}, bf16[128,1024]{1,0:T(8,128)(2,1)}, f32[4,2048]{1,0:T(4,128)}, /*index=5*/f32[31,2048]{1,0:T(8,128)}) custom-call(bf16[128,1024]{1,0:T(8,128)(2,1)} %bitcast.13, bf16[128,1024]{1,0:T(8,128)(2,1)} %bitcast.14, bf16[128,1024]{1,0:T(8,128)(2,1)} %bitcast.15, ...), custom_call_target="tpu_custom_call" | custom-call | tf_op jit(solution)/shard_map/pallas_call | solution.py:511
  117.5 0.0 copy-start.3
  117.5 1.9 %copy.18 = bf16[1,128,2048]{2,1,0:T(8,128)(2,1)} copy(bf16[1,128,2048]{2,1,0:T(8,128)(2,1)} %bitcast.8) | data formatting | bytes 1048576
  119.4 0.0 copy-done.3
  119.4 0.0 copy-start.2
  119.4 0.7 copy.19
  120.1 0.3 copy-done.2
  120.5 0.0 copy-start.1
  120.5 0.7 copy.20
  121.2 0.3 copy-done.1
  121.5 0.0 copy-start.4
  121.5 0.0 copy-start
  121.5 0.7 copy.21
  122.2 0.1 copy-done.4
  122.3 0.6 copy.22
  122.9 0.0 copy-done
  122.9 0.7 copy.23
Async XLA Ops:
  117.5 1.9 %copy-start.3 = (bf16[128,1024]{1,0:T(8,128)(2,1)S(1)}, bf16[128,1024]{1,0:T(8,128)(2,1)}, u32[]{:S(2)}) copy-start(bf16[128,1024]{1,0:T(8,128)(2,1)} %get-tuple-element.13) | copy-start | bytes 786436
  119.4 1.0 copy-start.2
  120.5 1.0 copy-start.1
  121.5 0.8 copy-start.4
  121.5 1.4 %copy-start = (f32[31,2048]{1,0:T(8,128)S(1)}, f32[31,2048]{1,0:T(8,128)}, u32[]{:S(2)}) copy-start(f32[31,2048]{1,0:T(8,128)} %get-tuple-element.29) | copy-start | bytes 761860

commit v2 on v1

v2 whole, which is shorter than its diff:
```python
import math

import jax
import jax.numpy as jnp
from jax import lax
from jax.experimental import pallas as pl
from jax.experimental.pallas import tpu as pltpu
from jax.sharding import PartitionSpec as P

MESH = pl.DeviceIdType.MESH
HDIM = 128
KERNEL = 31
ROWS = 128
INNER = 1024
D = 2048
SPAN = 1024
FS = 8
NZ = 8
NP = 16
HALO = 32
COLS = 256
PART = 512
BLK = 256
INV_ROOT = 1.0 / math.sqrt(HDIM)
EXP_SCALE = INV_ROOT * math.log2(math.e)
F32 = jnp.float32
BF16 = jnp.bfloat16


def mod(a, n):
    return lax.rem(a, jnp.int32(n))


def remote(src, dst, send, recv, device):
    return pltpu.make_async_remote_copy(
        src_ref=src, dst_ref=dst, send_sem=send, recv_sem=recv, device_id=device, device_id_type=MESH
    )


def loop(lower, upper, body):
    def step(i, carry):
        body(i)
        return carry

    lax.fori_loop(lower, upper, step, 0)


def at128(i):
    return pl.ds(pl.multiple_of(i * 128, 128), 128)


def at64(i):
    return pl.ds(pl.multiple_of(i * 64, 64), 64)


def dot_nt(a, b):
    return lax.dot_general(a, b, (((1,), (1,)), ((), ())), preferred_element_type=F32)


def dot_tn(a, b):
    return lax.dot_general(a, b, (((0,), (0,)), ((), ())), preferred_element_type=F32)


def kernel(
    q_ref, k_ref, v_ref, w_ref, taps_ref, go_ref,
    o_block, o_gq, o_gk, o_gv, o_wg, o_cg,
    qkvh, prob, ohp, attx, wpl, wtmp, wbuf, perm, attp, attt, gox, tapv, tapb, proj_s, next_s, gc_s, gp_s, last_s, wgs,
    ga_acc, ga_s, gh, dh, dk_acc, dv_acc, pbuf, sbuf, rbuf, wgp_s, wgp_r,
    tapg, ta, tp_s, tp_r, tb, tc_s, tc,
    own_s, qkv_ss, qkv_rs, wpl_ss, wpl_rs, go_ss, go_rs, ag_ss, ag_rs, agp_ss, agp_rs, att_ss, att_rs,
    ga_ss, ga_rs, rsp_ss, rsp_rs, rs_ss, rs_rs, d_ss, d_rs, wgp_ss, wgp_rs,
    ta_ss, ta_rs, tp_ss, tp_rs, tb_ss, tb_rs, tc_ss, tc_rs,
):
    f = lax.axis_index("fsdp").astype(jnp.int32)
    r = lax.axis_index("frame").astype(jnp.int32)
    ylo = lax.div(r, jnp.int32(16))
    z = mod(lax.div(r, jnp.int32(2)), NZ)
    core = mod(r, 2)
    me = f * 2 + ylo

    def plane(p):
        return (lax.div(p, jnp.int32(2)), mod(p, 2) * 16 + z * 2 + core)

    def zline(other):
        return (f, ylo * 16 + other * 2 + core)

    partner = (f, ylo * 16 + z * 2 + 1 - core)

    heads = ((q_ref, 0), (k_ref, 1), (v_ref, 2))

    def own_copies():
        for source, slot in heads:
            yield pltpu.make_async_copy(source.at[:, at128(f)], qkvh.at[slot, at128(f), :], own_s.at[slot])
        yield pltpu.make_async_copy(go_ref, gox.at[pl.ds(16, ROWS), :], own_s.at[3])
        yield pltpu.make_async_copy(w_ref, wpl.at[me], own_s.at[4])
        yield pltpu.make_async_copy(taps_ref, tapv, own_s.at[5])

    barrier = pltpu.get_barrier_semaphore()

    def greet_plane(k):
        pl.semaphore_signal(barrier, inc=1, device_id=plane(mod(me + k, NP)), device_id_type=MESH)

    def greet_z(k):
        pl.semaphore_signal(barrier, inc=1, device_id=zline(mod(z + k, NZ)), device_id_type=MESH)

    loop(1, NP, greet_plane)
    loop(1, NZ, greet_z)
    pl.semaphore_signal(barrier, inc=1, device_id=partner, device_id_type=MESH)
    for copy in own_copies():
        copy.start()

    @pl.when(f == 0)
    def _():
        gox[0:16, :] = jnp.zeros((16, D), BF16)

    @pl.when(f == FS - 1)
    def _():
        gox[144:160, :] = jnp.zeros((16, D), BF16)

    ohp[0:HALO, :] = jnp.zeros((HALO, HDIM), BF16)
    ohp[HALO + SPAN : HALO + SPAN + HALO, :] = jnp.zeros((HALO, HDIM), BF16)

    def perm_rows(b):
        row = lax.broadcasted_iota(jnp.int32, (128, INNER), 0) + b * 128
        col = lax.broadcasted_iota(jnp.int32, (128, INNER), 1)
        at = ((col >> 2) & 15) * 64 + ((col >> 6) & 7) * 8 + (col >> 9) * 4 + (col & 3)
        perm[at128(b), :] = jnp.where(row == at, 1.0, 0.0).astype(BF16)

    loop(0, 8, perm_rows)
    for copy in own_copies():
        copy.wait()
    taps = tapv[...].astype(F32)
    for j in range(KERNEL):
        tapb[j] = jnp.broadcast_to(taps[j : j + 1, :], (8, D))
    pl.semaphore_wait(barrier, NP - 1 + NZ - 1 + 1)

    def wpl_copy(k):
        return remote(w_ref, wpl.at[me], wpl_ss.at[k], wpl_rs.at[k], plane(mod(me + k, NP)))

    loop(1, NP, lambda k: wpl_copy(k).start())

    def qkv_copy(k, source, slot):
        peer = mod(f + k, FS)
        return remote(
            source.at[:, at128(peer)], qkvh.at[slot, at128(f), :], qkv_ss.at[slot, k], qkv_rs.at[slot, k], (peer, r)
        )

    def go_down():
        return remote(go_ref.at[pl.ds(0, 16), :], gox.at[pl.ds(144, 16), :], go_ss.at[0], go_rs.at[0], (f - 1, r))

    def go_up():
        return remote(go_ref.at[pl.ds(112, 16), :], gox.at[pl.ds(0, 16), :], go_ss.at[1], go_rs.at[1], (f + 1, r))

    for source, slot in heads[1:] + heads[:1]:
        loop(1, FS, lambda k: qkv_copy(k, source, slot).start())

    @pl.when(f > 0)
    def _():
        go_down().start()

    @pl.when(f < FS - 1)
    def _():
        go_up().start()

    def wpl_arrived(k):
        source = mod(me - k + NP, NP)
        remote(w_ref, wpl.at[source], wpl_ss.at[k], wpl_rs.at[k], plane(source)).wait_recv()

    loop(1, NP, wpl_arrived)
    for p in range(NP):
        wtmp[4 * p : 4 * p + 4, :] = wpl[p].astype(F32)

    def wblock(c, zz):
        return pl.ds(pl.multiple_of(c * 512 + zz * 64, 64), 64)

    wbuf[wblock(core, z), :] = wtmp[...].astype(BF16)

    up, down = zline(mod(z + 1, NZ)), zline(mod(z + NZ - 1, NZ))

    def ag_part(part):
        return pl.ds(part * PART, PART)

    def ag_copy(way, s, part):
        block = mod(z - s + NZ, NZ) if way == 0 else mod(z + s, NZ)
        view = wbuf.at[wblock(core, block), ag_part(part)]
        return remote(view, view, ag_ss.at[way, s, part], ag_rs.at[way, s, part], up if way == 0 else down)

    def ag_arrived(way, s, part):
        block = mod(z - 1 - s + NZ, NZ) if way == 0 else mod(z + 1 + s, NZ)
        view = wbuf.at[wblock(core, block), ag_part(part)]
        remote(view, view, ag_ss.at[way, s, part], ag_rs.at[way, s, part], down if way == 0 else up).wait_recv()

    def agp_copy(k, pair):
        view = wbuf.at[wblock(core, mod(z + k, NZ)), pl.ds(pair * 1024, 1024)]
        return remote(view, view, agp_ss.at[pair, k], agp_rs.at[pair, k], partner)

    def agp_arrived(k, pair):
        view = wbuf.at[wblock(1 - core, mod(z + k, NZ)), pl.ds(pair * 1024, 1024)]
        remote(view, view, agp_ss.at[pair, k], agp_rs.at[pair, k], partner).wait_recv()

    def goes_far(way, s, part):
        return s < 3 or part % 2 == way

    def ag_first(pair):
        for part in (2 * pair, 2 * pair + 1):
            for way in range(2):
                ag_copy(way, 0, part).start()
        agp_copy(0, pair).start()

    def ag_turn(s, pair):
        for part in (2 * pair, 2 * pair + 1):
            for way in range(2):
                if goes_far(way, s, part):
                    ag_arrived(way, s, part)
                    if s < 3 and goes_far(way, s + 1, part):
                        ag_copy(way, s + 1, part).start()
        if s < 3:
            agp_copy(NZ - 1 - s, pair).start()
            agp_copy(1 + s, pair).start()
        else:
            agp_copy(4, pair).start()

    ag_first(0)
    ag_turn(0, 0)

    def head_arrived(source, ref, slot):
        k = mod(f - source + FS, FS)
        remote(
            ref.at[:, at128(source)], qkvh.at[slot, at128(source), :], qkv_ss.at[slot, k], qkv_rs.at[slot, k], (source, r)
        ).wait_recv()

    for ref, slot in heads[1:]:
        loop(1, FS, lambda k: head_arrived(mod(f - k + FS, FS), ref, slot))

    def ext(i):
        return pl.ds(pl.multiple_of(i * ROWS, ROWS), ROWS + 2 * HALO)

    def att_copy(k):
        peer = mod(f + k, FS)
        return remote(ohp.at[ext(peer), :], attx.at[:, at128(f)], att_ss.at[k], att_rs.at[k], (peer, r))

    first = lax.div(f, jnp.int32(2))

    def att_send(i):
        for half in range(2):
            peer = mod(2 * (first + i) - 1 + half + FS, FS)

            @pl.when(peer != f)
            def _():
                att_copy(mod(peer - f + FS, FS)).start()

    def attend(i):
        block = mod(first + i, SPAN // BLK)
        for half in range(2):
            source = 2 * block + half

            @pl.when(source != f)
            def _():
                head_arrived(source, *heads[0])

        rows = pl.ds(pl.multiple_of(block * BLK, BLK), BLK)
        scores = dot_nt(qkvh[0, rows, :], qkvh[1])
        exponent = jnp.exp2((scores - jnp.max(scores, axis=1, keepdims=True)) * EXP_SCALE)
        rounded = (exponent * (1.0 / jnp.sum(exponent, axis=1, keepdims=True))).astype(BF16)
        prob[rows, :] = rounded
        attended = jnp.dot(rounded, qkvh[2], preferred_element_type=F32)
        ohp[pl.ds(pl.multiple_of(block * BLK + HALO, HALO), BLK), :] = attended.astype(BF16)

        @pl.when(i > 0)
        def _():
            att_send(i)

    def att_arrived(k):
        source = mod(f - k + FS, FS)
        remote(ohp.at[ext(source), :], attx.at[:, at128(source)], att_ss.at[k], att_rs.at[k], (source, r)).wait_recv()

    loop(0, SPAN // BLK, attend)
    att_send(SPAN // BLK)
    attx[:, at128(f)] = ohp[ext(f), :]
    ag_turn(1, 0)
    ag_first(1)
    ag_turn(2, 0)
    ag_turn(0, 1)
    ag_turn(3, 0)
    ag_turn(1, 1)

    @pl.when(f < FS - 1)
    def _():
        remote(go_ref.at[pl.ds(0, 16), :], gox.at[pl.ds(144, 16), :], go_ss.at[0], go_rs.at[0], (f + 1, r)).wait_recv()

    @pl.when(f > 0)
    def _():
        remote(go_ref.at[pl.ds(112, 16), :], gox.at[pl.ds(0, 16), :], go_ss.at[1], go_rs.at[1], (f - 1, r)).wait_recv()

    loop(1, FS, att_arrived)
    attp[...] = jnp.dot(attx[...], perm[...], preferred_element_type=F32).astype(BF16)
    attt[...] = attp[HALO : HALO + ROWS, :].T
    loop(0, NZ, lambda k: agp_arrived(k, 0))
    ga_acc[...] = jnp.zeros((ROWS, INNER), F32)
    tapg[KERNEL : KERNEL + 1, :] = jnp.zeros((1, D), F32)

    def rsp_copy(part):
        cols = pl.ds(pl.multiple_of(part * PART, PART), PART)
        rows = pl.ds(pl.multiple_of((1 - core) * 512, 512), 512)
        return remote(wgs.at[rows, cols], pbuf.at[:, cols], rsp_ss.at[part], rsp_rs.at[part], partner)

    def rsp_arrived(part):
        cols = pl.ds(part * PART, PART)
        rows = pl.ds(pl.multiple_of(core * 512, 512), 512)
        remote(wgs.at[rows, cols], pbuf.at[:, cols], rsp_ss.at[part], rsp_rs.at[part], partner).wait_recv()

    def ta_copy(k):
        peer = mod(me + k, NP)
        return remote(tapg.at[:, at128(peer)], ta.at[k], ta_ss.at[k], ta_rs.at[k], plane(peer))

    def ta_arrived(k):
        source = mod(me - k + NP, NP)
        remote(tapg.at[:, at128(source)], ta.at[k], ta_ss.at[k], ta_rs.at[k], plane(source)).wait_recv()

    def takes_part(way, s, part):
        return s > 0 or (part % 2 == 1) == (way == 0)

    def rs_copy(way, s, part):
        view = (way, s, slice(None), pl.ds(part * PART, PART))
        return remote(
            sbuf.at[view], rbuf.at[view], rs_ss.at[way, s, part], rs_rs.at[way, s, part], up if way == 0 else down
        )

    def rs_arrived(way, s, part):
        view = (way, s, slice(None), pl.ds(part * PART, PART))
        remote(
            sbuf.at[view], rbuf.at[view], rs_ss.at[way, s, part], rs_rs.at[way, s, part], down if way == 0 else up
        ).wait_recv()

    def chip_sum(block, cols):
        return wgs[wblock(core, block), cols].astype(F32) + pbuf[at64(block), cols].astype(F32)

    def rs(s, part):
        cols = slice(part * PART, part * PART + PART)
        if s == 0:
            rsp_arrived(part)
        for way in range(2):
            if not takes_part(way, s, part):
                continue
            block = mod(z + 4 - s, NZ) if way == 0 else mod(z + 4 + s, NZ)
            value = chip_sum(block, cols)
            if s > 0 and takes_part(way, s - 1, part):
                rs_arrived(way, s - 1, part)
                value = value + rbuf[way, s - 1, :, cols].astype(F32)
            sbuf[way, s, :, cols] = value.astype(BF16)
            rs_copy(way, s, part).start()

    def at_cols(c):
        return pl.ds(pl.multiple_of(c * COLS, COLS), COLS)

    def project(c):
        next_s[...] = jnp.dot(attp[...], wbuf[:, at_cols(c)], preferred_element_type=F32).astype(BF16).astype(F32)

    def pull_back(c):
        gp = last_s[...]
        wgs[:, at_cols(c)] = jnp.dot(attt[...], gp, preferred_element_type=F32).astype(BF16)
        ga_acc[...] += dot_nt(gp, wbuf[:, at_cols(c)])

    events = {
        1: ((ag_turn, 2, 1),),
        2: ((ag_turn, 3, 1),),
        3: ((rs, 0, 0),),
        5: ((rs, 1, 0), (rs, 0, 1)),
        7: ((rs, 2, 0), (rs, 1, 1), (rs, 0, 2)),
    }

    def columns(c):
        project(jnp.minimum(c + 1, D // COLS - 1))
        pull_back(jnp.maximum(c - 1, 0))
        for lane in range(COLS // 128):
            here = pl.ds(pl.multiple_of(c * COLS + lane * 128, 128), 128)
            local = slice(lane * 128, lane * 128 + 128)
            conv = jnp.zeros((20, 8, 128), F32)
            for shift in range(8):
                moved = proj_s[shift : shift + 184, local]
                for j in range(KERNEL):
                    if (1 + j) % 8 == shift:
                        start = 1 + j - shift
                        conv = conv + tapb[j, :, here][None] * moved[start : start + 160].reshape(20, 8, 128)
            conv = conv.reshape(160, 128)
            sig = jax.nn.sigmoid(conv)
            upstream = gox[:, here].astype(F32)
            o_block[:, here] = (proj_s[32:160, local] + conv[16:144] * sig[16:144]).astype(BF16)
            gc_s[:, local] = (upstream * sig * (1.0 + conv * (1.0 - sig))).astype(BF16).astype(F32)
            total = gox[16:144, here].astype(F32).reshape(16, 8, 128)
            for shift in range(8):
                moved = gc_s[shift : shift + 152, local]
                for j in range(KERNEL):
                    if (31 - j) % 8 == shift:
                        start = 31 - j - shift
                        total = total + tapb[j, :, here][None] * moved[start : start + 128].reshape(16, 8, 128)
            gp_s[:, local] = total.reshape(128, 128).astype(BF16)
            gc_own = gc_s[16:144, local].reshape(16, 8, 128)
            for shift in range(8):
                moved = proj_s[shift : shift + 184, local]
                for j in range(KERNEL):
                    if (17 + j) % 8 == shift:
                        start = 17 + j - shift
                        partial = jnp.sum(gc_own * moved[start : start + 128].reshape(16, 8, 128), axis=0)
                        tapg[j : j + 1, here] = jnp.sum(partial, axis=0, keepdims=True)
        proj_s[...] = next_s[...]
        last_s[...] = gp_s[...]

        @pl.when((c > 0) & (mod(c, 2) == 0))
        def _():
            rsp_copy(lax.div(c, jnp.int32(2)) - 1).start()

        @pl.when(mod(c, 2) == 1)
        def _():
            for i in range(4):
                peer = lax.div(c, jnp.int32(2)) * 4 + i

                @pl.when(peer != me)
                def _():
                    ta_copy(mod(peer - me + NP, NP)).start()

        for at, calls in events.items():

            @pl.when(c == at)
            def _():
                for call, *given in calls:
                    call(*given)

        @pl.when(c == 2)
        def _():
            loop(0, NZ, lambda k: agp_arrived(k, 1))

    project(0)
    proj_s[...] = next_s[...]
    last_s[...] = jnp.zeros((ROWS, COLS), BF16)
    loop(0, D // COLS, columns)
    pull_back(D // COLS - 1)
    rsp_copy(3).start()
    ga_s[...] = dot_nt(ga_acc[...].astype(BF16), perm[...]).astype(BF16)

    def ga_copy(k):
        peer = mod(f + k, FS)
        return remote(ga_s.at[:, at128(peer)], gh.at[at128(f), :], ga_ss.at[k], ga_rs.at[k], (peer, r))

    def ga_arrived(k):
        source = mod(f - k + FS, FS)
        remote(ga_s.at[:, at128(source)], gh.at[at128(source), :], ga_ss.at[k], ga_rs.at[k], (source, r)).wait_recv()

    loop(1, FS, lambda k: ga_copy(k).start())

    gh[at128(f), :] = ga_s[:, at128(f)]
    rs(3, 0)
    rs(2, 1)
    rs(1, 2)
    rs(0, 3)
    loop(1, FS, ga_arrived)
    dk_acc[...] = jnp.zeros((SPAN, HDIM), F32)
    dv_acc[...] = jnp.zeros((SPAN, HDIM), F32)

    outs = ((o_gq, 0), (o_gk, 1), (o_gv, 2))

    def d_copy(k, ref, slot):
        peer = mod(f + k, FS)
        return remote(dh.at[slot, at128(peer), :], ref.at[:, at128(f)], d_ss.at[slot, k], d_rs.at[slot, k], (peer, r))

    def attend_back(i):
        i = mod(i + lax.div(f, jnp.int32(2)), SPAN // BLK)
        rows = pl.ds(pl.multiple_of(i * BLK, BLK), BLK)
        grad = gh[rows, :]
        rounded = prob[rows, :]
        weights = rounded.astype(F32)
        grad_probs = dot_nt(grad, qkvh[2])
        row_dot = jnp.sum(weights * grad_probs, axis=1, keepdims=True)
        grad_scores = (weights * (grad_probs - row_dot)).astype(BF16)
        dh[0, rows, :] = (jnp.dot(grad_scores, qkvh[1], preferred_element_type=F32) * INV_ROOT).astype(BF16)
        for half in range(2):
            peer = 2 * i + half

            @pl.when(peer != f)
            def _():
                d_copy(mod(peer - f + FS, FS), o_gq, 0).start()

        dk_acc[...] += dot_tn(grad_scores, qkvh[0, rows, :])
        dv_acc[...] += dot_tn(rounded, grad)

    def tp_copy():
        return remote(tp_s, tp_r, tp_ss, tp_rs, partner)

    def tb_copy(k):
        return remote(tb.at[z], tb.at[z], tb_ss.at[k], tb_rs.at[k], zline(mod(z + k, NZ)))

    def tb_arrived(k):
        source = mod(z - k + NZ, NZ)
        remote(tb.at[source], tb.at[source], tb_ss.at[k], tb_rs.at[k], zline(source)).wait_recv()

    def tc_copy(k):
        return remote(tc_s, tc.at[me], tc_ss.at[k], tc_rs.at[k], plane(mod(me + k, NP)))

    def tc_arrived(k):
        source = mod(me - k + NP, NP)
        remote(tc_s, tc.at[source], tc_ss.at[k], tc_rs.at[k], plane(source)).wait_recv()

    grad_scale = 1.0 / math.sqrt(SPAN * 32)

    def wgp_copy(half, k):
        peer = mod(me + k, NP)
        return remote(wgp_s.at[half, peer], wgp_r.at[half, k], wgp_ss.at[half, k], wgp_rs.at[half, k], plane(peer))

    def wgp_arrived(half, k):
        source = mod(me - k + NP, NP)
        remote(
            wgp_s.at[half, source], wgp_r.at[half, k], wgp_ss.at[half, k], wgp_rs.at[half, k], plane(source)
        ).wait_recv()

    def settle(half):
        for part in (2 * half, 2 * half + 1):
            cols = slice(part * PART, part * PART + PART)
            rs_arrived(0, 3, part)
            rs_arrived(1, 3, part)
            wtmp[:, cols] = chip_sum(z, cols) + rbuf[0, 3, :, cols].astype(F32) + rbuf[1, 3, :, cols].astype(F32)
        for p in range(NP):
            wgp_s[half, p] = wtmp[4 * p : 4 * p + 4, half * 1024 : half * 1024 + 1024].astype(BF16)
        loop(1, NP, lambda k: wgp_copy(half, k).start())

    loop(1, NP, ta_arrived)
    total = tapg[:, at128(me)]
    for k in range(1, NP):
        total = total + ta[k]
    tp_s[...] = total
    tp_copy().start()
    loop(0, 2, attend_back)
    rs(3, 1)
    rs(2, 2)
    rs(1, 3)
    tp_copy().wait_recv()
    tb[z] = tp_s[...] + tp_r[...]
    loop(1, NZ, lambda k: tb_copy(k).start())
    loop(2, 4, attend_back)
    dh[1] = (dk_acc[...] * INV_ROOT).astype(BF16)
    dh[2] = dv_acc[...].astype(BF16)

    def d_start(k):
        d_copy(k, o_gk, 1).start()
        d_copy(k, o_gv, 2).start()

    def d_arrived(k):
        source = mod(f - k + FS, FS)
        for ref, slot in outs:
            remote(
                dh.at[slot, at128(source), :], ref.at[:, at128(source)], d_ss.at[slot, k], d_rs.at[slot, k], (source, r)
            ).wait_recv()

    loop(1, FS, d_start)
    for ref, slot in outs:
        ref[:, at128(f)] = dh[slot, at128(f), :]
    rs(3, 2)
    rs(2, 3)
    loop(1, NZ, tb_arrived)
    total = tb[0]
    for k in range(1, NZ):
        total = total + tb[k]
    tc_s[...] = total * grad_scale
    loop(1, NP, lambda k: tc_copy(k).start())
    tc[me] = tc_s[...]
    settle(0)
    rs(3, 3)
    settle(1)
    loop(1, NP, tc_arrived)
    for p in range(NP):
        o_cg[:, p * 128 : p * 128 + 128] = tc[p, 0:KERNEL, :]
    loop(1, FS, d_arrived)
    for half in range(2):
        loop(1, NP, lambda k: wgp_arrived(half, k))
        total = wgp_s[half, me].astype(F32)
        for k in range(1, NP):
            total = total + wgp_r[half, k].astype(F32)
        o_wg[:, half * 1024 : half * 1024 + 1024] = total * grad_scale

    def plane_sent(k):
        wpl_copy(k).wait_send()
        ta_copy(k).wait_send()
        tc_copy(k).wait_send()
        for half in range(2):
            wgp_copy(half, k).wait_send()

    def span_sent(k):
        for ref, slot in heads:
            qkv_copy(k, ref, slot).wait_send()
        for ref, slot in outs:
            d_copy(k, ref, slot).wait_send()
        att_copy(k).wait_send()
        ga_copy(k).wait_send()

    loop(1, NP, plane_sent)
    loop(1, FS, span_sent)

    @pl.when(f > 0)
    def _():
        go_down().wait_send()

    @pl.when(f < FS - 1)
    def _():
        go_up().wait_send()

    for way in range(2):
        for s in range(4):
            for part in range(4):
                if goes_far(way, s, part):
                    ag_copy(way, s, part).wait_send()
                if takes_part(way, s, part):
                    rs_copy(way, s, part).wait_send()
    for part in range(4):
        rsp_copy(part).wait_send()
    for pair in range(2):
        loop(0, NZ, lambda k: agp_copy(k, pair).wait_send())
    loop(1, NZ, lambda k: tb_copy(k).wait_send())
    tp_copy().wait_send()


def put_out(*refs):
    sources, targets, rooms, into, out = refs[:6], refs[6:12], refs[12:18], refs[18], refs[19]
    loads = [pltpu.make_async_copy(sources[i], rooms[i], into.at[i]) for i in range(6)]
    stores = [pltpu.make_async_copy(rooms[i], targets[i], out.at[i]) for i in range(6)]
    for load in loads:
        load.start()
    for load, store in zip(loads, stores):
        load.wait()
        store.start()
    for store in stores:
        store.wait()


def shards(queries, key_rows, value_rows, out_weight, conv_weight, grad_out):
    vmem = pl.BlockSpec(memory_space=pltpu.VMEM)
    hbm = pl.BlockSpec(memory_space=pltpu.HBM)
    anywhere = pl.BlockSpec(memory_space=pl.ANY)
    dma = pltpu.SemaphoreType.DMA
    results = (
        ((ROWS, D), BF16),
        ((ROWS, INNER), BF16),
        ((ROWS, INNER), BF16),
        ((ROWS, INNER), BF16),
        ((4, D), F32),
        ((KERNEL, D), F32),
    )
    shapes = tuple(jax.ShapeDtypeStruct(*result) for result in results)
    found = pl.pallas_call(
        kernel,
        out_shape=shapes,
        in_specs=[hbm] * 6,
        out_specs=(vmem,) * 6,
        scratch_shapes=[
            pltpu.VMEM((3, SPAN, HDIM), BF16),
            pltpu.VMEM((SPAN, SPAN), BF16),
            pltpu.VMEM((SPAN + 2 * HALO, HDIM), BF16),
            pltpu.VMEM((ROWS + 2 * HALO, INNER), BF16),
            pltpu.VMEM((NP, 4, D), BF16),
            pltpu.VMEM((64, D), F32),
            pltpu.VMEM((INNER, D), BF16),
            pltpu.VMEM((INNER, INNER), BF16),
            pltpu.VMEM((ROWS + 2 * HALO, INNER), BF16),
            pltpu.VMEM((INNER, ROWS), BF16),
            pltpu.VMEM((160, D), BF16),
            pltpu.VMEM((KERNEL, D), BF16),
            pltpu.VMEM((KERNEL, 8, D), F32),
            pltpu.VMEM((ROWS + 2 * HALO, COLS), F32),
            pltpu.VMEM((ROWS + 2 * HALO, COLS), F32),
            pltpu.VMEM((160, COLS), F32),
            pltpu.VMEM((ROWS, COLS), BF16),
            pltpu.VMEM((ROWS, COLS), BF16),
            pltpu.VMEM((INNER, D), BF16),
            pltpu.VMEM((ROWS, INNER), F32),
            pltpu.VMEM((ROWS, INNER), BF16),
            pltpu.VMEM((SPAN, HDIM), BF16),
            pltpu.VMEM((3, SPAN, HDIM), BF16),
            pltpu.VMEM((SPAN, HDIM), F32),
            pltpu.VMEM((SPAN, HDIM), F32),
            pltpu.VMEM((512, D), BF16),
            pltpu.VMEM((2, 4, 64, D), BF16),
            pltpu.VMEM((2, 4, 64, D), BF16),
            pltpu.VMEM((2, NP, 4, 1024), BF16),
            pltpu.VMEM((2, NP, 4, 1024), BF16),
            pltpu.VMEM((32, D), F32),
            pltpu.VMEM((NP, 32, 128), F32),
            pltpu.VMEM((32, 128), F32),
            pltpu.VMEM((32, 128), F32),
            pltpu.VMEM((NZ, 32, 128), F32),
            pltpu.VMEM((32, 128), F32),
            pltpu.VMEM((NP, 32, 128), F32),
            dma((6,)),
            dma((3, FS)), dma((3, FS)),
            dma((NP,)), dma((NP,)),
            dma((2,)), dma((2,)),
            dma((2, 4, 4)), dma((2, 4, 4)),
            dma((2, NZ)), dma((2, NZ)),
            dma((FS,)), dma((FS,)),
            dma((FS,)), dma((FS,)),
            dma((4,)), dma((4,)),
            dma((2, 4, 4)), dma((2, 4, 4)),
            dma((3, FS)), dma((3, FS)),
            dma((2, NP)), dma((2, NP)),
            dma((NP,)), dma((NP,)),
            dma, dma,
            dma((NZ,)), dma((NZ,)),
            dma((NP,)), dma((NP,)),
        ],
        compiler_params=pltpu.CompilerParams(
            collective_id=0, has_side_effects=True, vmem_limit_bytes=50 * 1024 * 1024
        ),
    )(
        *(
            pltpu.with_memory_space_constraint(given, pltpu.HBM)
            for given in (queries[0], key_rows[0], value_rows[0], out_weight, conv_weight, grad_out[0])
        )
    )
    block_out, grad_queries, grad_keys, grad_values, weight_grad, conv_grad = pl.pallas_call(
        put_out,
        out_shape=shapes,
        in_specs=[anywhere] * 6,
        out_specs=(hbm,) * 6,
        scratch_shapes=[pltpu.VMEM(*result) for result in results] + [dma((6,)), dma((6,))],
        compiler_params=pltpu.CompilerParams(vmem_limit_bytes=8 * 1024 * 1024),
    )(*found)
    return (block_out[None], grad_queries[None], grad_keys[None], grad_values[None], weight_grad, conv_grad)


def solution(mesh):
    return jax.shard_map(
        shards,
        mesh=mesh,
        in_specs=(
            P("frame", "fsdp", None),
            P("frame", "fsdp", None),
            P("frame", "fsdp", None),
            P(("fsdp", "frame"), None),
            P(),
            P("frame", "fsdp", None),
        ),
        out_specs=(
            P("frame", "fsdp", None),
            P("frame", "fsdp", None),
            P("frame", "fsdp", None),
            P("frame", "fsdp", None),
            P(("fsdp", "frame"), None),
            P(),
        ),
        check_vma=False,
    )
```

time: 124 us -> 102 us (0.82)
  Pallas kernels: 117 us -> 101 us
  local copies, waits for them, and re-layouts: 6.09 us -> 0 us
    pallas_call x1 -> x2, Pallas kernels: 117 us -> 101 us  [the longest x1 99.1 us: shards(): pl.pallas_call(kernel, out_shape=shapes, in_specs=[hbm] * 6, out_specs=(v...]
    unnamed x16 -> x0, local copies, waits for them, and re-layouts: 6.09 us -> none
where the time goes in v2:
time: 102 us; the launch traced here: 101 us
  Pallas kernels  101 us (99%)
    pallas_call x1, Pallas kernels, shards(): pl.pallas_call(kernel, out_shape=shapes, in_specs=[hbm] * 6, out_specs=(v...  99.1 us

profile of v2, /device:TPU:8, one launch (start us, length us, event | category | flops | bytes accessed | tf_op | source)
XLA Modules:
  0.0 101.2 jit_solution(8019187376158026346)
XLA Ops:
  0.6 99.1 %shard_map.109 = (bf16[128,2048]{1,0:T(8,128)(2,1)S(1)}, bf16[128,1024]{1,0:T(8,128)(2,1)S(1)}, bf16[128,1024]{1,0:T(8,128)(2,1)S(1)}, bf16[128,1024]{1,0:T(8,12...) custom-call(bf16[128,1024]{1,0:T(8,128)(2,1)} %bitcast.9, bf16[128,1024]{1,0:T(8,128)(2,1)} %bitcast.10, ...), custom_call_target="tpu_custom_call" | custom-call | tf_op jit(solution)/shard_map/pallas_call | solution.py:647
  99.8 1.4 %shard_map.110 = (bf16[128,2048]{1,0:T(8,128)(2,1)}, bf16[128,1024]{1,0:T(8,128)(2,1)}, bf16[128,1024]{1,0:T(8,128)(2,1)}, bf16[128,1024]{1,0:T(8,128)(2,1)}, f32[4,2048]{1,0:T(4,128)}, /*index=5*/f32[31,2048]{1,0:T(8,128)}) custom-call(bf16[128,2048]{1,0:T(8,128)(2,1)S(1)} %get-tuple-element.18.refs_0_, bf16[128,1024]{1,0:T(8,128)(2,1)S(1)} %get-tuple-element.19.refs_1_, ...), custom_call_target="tpu_custom_call" | custom-call | tf_op jit(solution)/shard_map/pallas_call | solution.py:716

commit v3 on v2

--- a/solution.py
+++ b/solution.py
@@ -64,10 +64,10 @@
 def kernel(
     q_ref, k_ref, v_ref, w_ref, taps_ref, go_ref,
     o_block, o_gq, o_gk, o_gv, o_wg, o_cg,
-    qkvh, prob, ohp, attx, wpl, wtmp, wbuf, perm, attp, attt, gox, tapv, tapb, proj_s, next_s, gc_s, gp_s, last_s, wgs,
+    qkvh, prob, ohp, attx, wpl, wtmp, wbuf, perm, attp, attt, gox, tapv, tapb, proj_s, next_s, proj_all, gc_s, gc_all, gp_s, last_s, wgs,
     ga_acc, ga_s, gh, dh, dk_acc, dv_acc, pbuf, sbuf, rbuf, wgp_s, wgp_r,
     tapg, ta, tp_s, tp_r, tb, tc_s, tc,
-    own_s, qkv_ss, qkv_rs, wpl_ss, wpl_rs, go_ss, go_rs, ag_ss, ag_rs, agp_ss, agp_rs, att_ss, att_rs,
+    own_s, qkv_ss, q_rs, kv_rs, wpl_ss, wpl_rs, go_ss, go_rs, ag_ss, ag_rs, agp_ss, agp_rs, att_ss, att_rs,
     ga_ss, ga_rs, rsp_ss, rsp_rs, rs_ss, rs_rs, d_ss, d_rs, wgp_ss, wgp_rs,
     ta_ss, ta_rs, tp_ss, tp_rs, tb_ss, tb_rs, tc_ss, tc_rs,
 ):
@@ -86,6 +86,12 @@
 
     partner = (f, ylo * 16 + z * 2 + 1 - core)
 
+    def all_arrived(ref, sem):
+        remote(ref, ref, sem, sem, partner).wait_recv()
+
+    def all_sent(ref, sem):
+        remote(ref, ref, sem, sem, partner).wait_send()
+
     heads = ((q_ref, 0), (k_ref, 1), (v_ref, 2))
 
     def own_copies():
@@ -135,15 +141,14 @@
     pl.semaphore_wait(barrier, NP - 1 + NZ - 1 + 1)
 
     def wpl_copy(k):
-        return remote(w_ref, wpl.at[me], wpl_ss.at[k], wpl_rs.at[k], plane(mod(me + k, NP)))
+        return remote(w_ref, wpl.at[me], wpl_ss, wpl_rs, plane(mod(me + k, NP)))
 
     loop(1, NP, lambda k: wpl_copy(k).start())
 
     def qkv_copy(k, source, slot):
         peer = mod(f + k, FS)
-        return remote(
-            source.at[:, at128(peer)], qkvh.at[slot, at128(f), :], qkv_ss.at[slot, k], qkv_rs.at[slot, k], (peer, r)
-        )
+        arrival = q_rs.at[k] if slot == 0 else kv_rs.at[slot - 1]
+        return remote(source.at[:, at128(peer)], qkvh.at[slot, at128(f), :], qkv_ss, arrival, (peer, r))
 
     def go_down():
         return remote(go_ref.at[pl.ds(0, 16), :], gox.at[pl.ds(144, 16), :], go_ss.at[0], go_rs.at[0], (f - 1, r))
@@ -151,22 +156,8 @@
     def go_up():
         return remote(go_ref.at[pl.ds(112, 16), :], gox.at[pl.ds(0, 16), :], go_ss.at[1], go_rs.at[1], (f + 1, r))
 
-    for source, slot in heads[1:] + heads[:1]:
-        loop(1, FS, lambda k: qkv_copy(k, source, slot).start())
-
-    @pl.when(f > 0)
-    def _():
-        go_down().start()
-
-    @pl.when(f < FS - 1)
-    def _():
-        go_up().start()
-
-    def wpl_arrived(k):
-        source = mod(me - k + NP, NP)
-        remote(w_ref, wpl.at[source], wpl_ss.at[k], wpl_rs.at[k], plane(source)).wait_recv()
-
-    loop(1, NP, wpl_arrived)
+    loop(1, FS, lambda k: qkv_copy(k, k_ref, 1).start())
+    all_arrived(wpl.at[pl.ds(0, NP - 1)], wpl_rs)
     for p in range(NP):
         wtmp[4 * p : 4 * p + 4, :] = wpl[p].astype(F32)
 
@@ -183,61 +174,70 @@
     def ag_copy(way, s, part):
         block = mod(z - s + NZ, NZ) if way == 0 else mod(z + s, NZ)
         view = wbuf.at[wblock(core, block), ag_part(part)]
-        return remote(view, view, ag_ss.at[way, s, part], ag_rs.at[way, s, part], up if way == 0 else down)
+        return remote(view, view, ag_ss, ag_rs.at[way, s, part], up if way == 0 else down)
 
     def ag_arrived(way, s, part):
         block = mod(z - 1 - s + NZ, NZ) if way == 0 else mod(z + 1 + s, NZ)
         view = wbuf.at[wblock(core, block), ag_part(part)]
-        remote(view, view, ag_ss.at[way, s, part], ag_rs.at[way, s, part], down if way == 0 else up).wait_recv()
-
-    def agp_copy(k, pair):
-        view = wbuf.at[wblock(core, mod(z + k, NZ)), pl.ds(pair * 1024, 1024)]
-        return remote(view, view, agp_ss.at[pair, k], agp_rs.at[pair, k], partner)
-
-    def agp_arrived(k, pair):
-        view = wbuf.at[wblock(1 - core, mod(z + k, NZ)), pl.ds(pair * 1024, 1024)]
-        remote(view, view, agp_ss.at[pair, k], agp_rs.at[pair, k], partner).wait_recv()
+        remote(view, view, ag_ss, ag_rs.at[way, s, part], down if way == 0 else up).wait_recv()
+
+    def agp_copy(k, part):
+        view = wbuf.at[wblock(core, mod(z + k, NZ)), ag_part(part)]
+        return remote(view, view, agp_ss, agp_rs.at[part], partner)
 
     def goes_far(way, s, part):
         return s < 3 or part % 2 == way
 
-    def ag_first(pair):
-        for part in (2 * pair, 2 * pair + 1):
+    def ag_first(*parts):
+        for part in parts:
             for way in range(2):
                 ag_copy(way, 0, part).start()
-        agp_copy(0, pair).start()
-
-    def ag_turn(s, pair):
-        for part in (2 * pair, 2 * pair + 1):
+        for part in parts:
+            agp_copy(0, part).start()
+
+    def ag_turn(s, *parts):
+        for part in parts:
             for way in range(2):
                 if goes_far(way, s, part):
                     ag_arrived(way, s, part)
                     if s < 3 and goes_far(way, s + 1, part):
                         ag_copy(way, s + 1, part).start()
-        if s < 3:
-            agp_copy(NZ - 1 - s, pair).start()
-            agp_copy(1 + s, pair).start()
-        else:
-            agp_copy(4, pair).start()
-
-    ag_first(0)
-    ag_turn(0, 0)
-
-    def head_arrived(source, ref, slot):
-        k = mod(f - source + FS, FS)
-        remote(
-            ref.at[:, at128(source)], qkvh.at[slot, at128(source), :], qkv_ss.at[slot, k], qkv_rs.at[slot, k], (source, r)
-        ).wait_recv()
-
-    for ref, slot in heads[1:]:
-        loop(1, FS, lambda k: head_arrived(mod(f - k + FS, FS), ref, slot))
+            if s < 3:
+                agp_copy(NZ - 1 - s, part).start()
+                agp_copy(1 + s, part).start()
+            else:
+                agp_copy(4, part).start()
+
+    def agp_arrived(part):
+        all_arrived(wbuf.at[pl.ds(0, 512), ag_part(part)], agp_rs.at[part])
+
+    ag_first(0, 1, 2)
+    loop(1, FS, lambda k: qkv_copy(k, v_ref, 2).start())
+    loop(1, FS, lambda k: qkv_copy(k, q_ref, 0).start())
+
+    @pl.when(f > 0)
+    def _():
+        go_down().start()
+
+    @pl.when(f < FS - 1)
+    def _():
+        go_up().start()
+
+    ag_turn(0, 0, 1, 2)
+
+    def query_arrived(source):
+        arrival = q_rs.at[mod(f - source + FS, FS)]
+        remote(q_ref.at[:, at128(source)], qkvh.at[0, at128(source), :], qkv_ss, arrival, (source, r)).wait_recv()
+
+    for slot in (1, 2):
+        all_arrived(qkvh.at[slot, pl.ds(0, 896), :], kv_rs.at[slot - 1])
 
     def ext(i):
         return pl.ds(pl.multiple_of(i * ROWS, ROWS), ROWS + 2 * HALO)
 
     def att_copy(k):
         peer = mod(f + k, FS)
-        return remote(ohp.at[ext(peer), :], attx.at[:, at128(f)], att_ss.at[k], att_rs.at[k], (peer, r))
+        return remote(ohp.at[ext(peer), :], attx.at[:, at128(f)], att_ss, att_rs, (peer, r))
 
     first = lax.div(f, jnp.int32(2))
 
@@ -256,7 +256,7 @@
 
             @pl.when(source != f)
             def _():
-                head_arrived(source, *heads[0])
+                query_arrived(source)
 
         rows = pl.ds(pl.multiple_of(block * BLK, BLK), BLK)
         scores = dot_nt(qkvh[0, rows, :], qkvh[1])
@@ -270,19 +270,19 @@
         def _():
             att_send(i)
 
-    def att_arrived(k):
-        source = mod(f - k + FS, FS)
-        remote(ohp.at[ext(source), :], attx.at[:, at128(source)], att_ss.at[k], att_rs.at[k], (source, r)).wait_recv()
+        for part in range(3):
+
+            @pl.when(i == part)
+            def _():
+                ag_turn(1, part)
 
     loop(0, SPAN // BLK, attend)
     att_send(SPAN // BLK)
     attx[:, at128(f)] = ohp[ext(f), :]
-    ag_turn(1, 0)
-    ag_first(1)
-    ag_turn(2, 0)
-    ag_turn(0, 1)
-    ag_turn(3, 0)
-    ag_turn(1, 1)
+    ag_turn(2, 0, 1, 2)
+    ag_first(3)
+    ag_turn(3, 0, 1, 2)
+    ag_turn(0, 3)
 
     @pl.when(f < FS - 1)
     def _():
@@ -292,30 +292,26 @@
     def _():
         remote(go_ref.at[pl.ds(112, 16), :], gox.at[pl.ds(0, 16), :], go_ss.at[1], go_rs.at[1], (f - 1, r)).wait_recv()
 
-    loop(1, FS, att_arrived)
+    all_arrived(attx.at[:, pl.ds(0, 896)], att_rs)
     attp[...] = jnp.dot(attx[...], perm[...], preferred_element_type=F32).astype(BF16)
     attt[...] = attp[HALO : HALO + ROWS, :].T
-    loop(0, NZ, lambda k: agp_arrived(k, 0))
+    agp_arrived(0)
     ga_acc[...] = jnp.zeros((ROWS, INNER), F32)
     tapg[KERNEL : KERNEL + 1, :] = jnp.zeros((1, D), F32)
 
     def rsp_copy(part):
         cols = pl.ds(pl.multiple_of(part * PART, PART), PART)
         rows = pl.ds(pl.multiple_of((1 - core) * 512, 512), 512)
-        return remote(wgs.at[rows, cols], pbuf.at[:, cols], rsp_ss.at[part], rsp_rs.at[part], partner)
+        return remote(wgs.at[rows, cols], pbuf.at[:, cols], rsp_ss, rsp_rs.at[part], partner)
 
     def rsp_arrived(part):
         cols = pl.ds(part * PART, PART)
         rows = pl.ds(pl.multiple_of(core * 512, 512), 512)
-        remote(wgs.at[rows, cols], pbuf.at[:, cols], rsp_ss.at[part], rsp_rs.at[part], partner).wait_recv()
+        remote(wgs.at[rows, cols], pbuf.at[:, cols], rsp_ss, rsp_rs.at[part], partner).wait_recv()
 
     def ta_copy(k):
         peer = mod(me + k, NP)
-        return remote(tapg.at[:, at128(peer)], ta.at[k], ta_ss.at[k], ta_rs.at[k], plane(peer))
-
-    def ta_arrived(k):
-        source = mod(me - k + NP, NP)
-        remote(tapg.at[:, at128(source)], ta.at[k], ta_ss.at[k], ta_rs.at[k], plane(source)).wait_recv()
+        return remote(tapg.at[:, at128(peer)], ta.at[k], ta_ss, ta_rs, plane(peer))
 
     def takes_part(way, s, part):
         return s > 0 or (part % 2 == 1) == (way == 0)
@@ -323,13 +319,13 @@
     def rs_copy(way, s, part):
         view = (way, s, slice(None), pl.ds(part * PART, PART))
         return remote(
-            sbuf.at[view], rbuf.at[view], rs_ss.at[way, s, part], rs_rs.at[way, s, part], up if way == 0 else down
+            sbuf.at[view], rbuf.at[view], rs_ss, rs_rs.at[way, s, part], up if way == 0 else down
         )
 
     def rs_arrived(way, s, part):
         view = (way, s, slice(None), pl.ds(part * PART, PART))
         remote(
-            sbuf.at[view], rbuf.at[view], rs_ss.at[way, s, part], rs_rs.at[way, s, part], down if way == 0 else up
+            sbuf.at[view], rbuf.at[view], rs_ss, rs_rs.at[way, s, part], down if way == 0 else up
         ).wait_recv()
 
     def chip_sum(block, cols):
@@ -362,12 +358,29 @@
         ga_acc[...] += dot_nt(gp, wbuf[:, at_cols(c)])
 
     events = {
-        1: ((ag_turn, 2, 1),),
-        2: ((ag_turn, 3, 1),),
+        0: ((ag_turn, 1, 3), (agp_arrived, 1)),
+        2: ((ag_turn, 2, 3), (agp_arrived, 2)),
         3: ((rs, 0, 0),),
-        5: ((rs, 1, 0), (rs, 0, 1)),
-        7: ((rs, 2, 0), (rs, 1, 1), (rs, 0, 2)),
+        4: ((ag_turn, 3, 3), (agp_arrived, 3)),
+        5: ((rs, 0, 1),),
+        6: ((rs, 1, 0),),
+        7: ((rs, 0, 2),),
     }
+
+    def tap_grads(tile):
+        here = at128(tile)
+        gc_own = gc_all[:, here].reshape(16, 8, 128)
+        for shift in range(8):
+            moved = proj_all[shift : shift + 184, here]
+            for j in range(KERNEL):
+                if (17 + j) % 8 == shift:
+                    start = 17 + j - shift
+                    partial = jnp.sum(gc_own * moved[start : start + 128].reshape(16, 8, 128), axis=0)
+                    tapg[j : j + 1, here] = jnp.sum(partial, axis=0, keepdims=True)
+
+        @pl.when(tile != me)
+        def _():
+            ta_copy(mod(tile - me + NP, NP)).start()
 
     def columns(c):
         project(jnp.minimum(c + 1, D // COLS - 1))
@@ -386,7 +399,9 @@
             sig = jax.nn.sigmoid(conv)
             upstream = gox[:, here].astype(F32)
             o_block[:, here] = (proj_s[32:160, local] + conv[16:144] * sig[16:144]).astype(BF16)
-            gc_s[:, local] = (upstream * sig * (1.0 + conv * (1.0 - sig))).astype(BF16).astype(F32)
+            grad_conv = (upstream * sig * (1.0 + conv * (1.0 - sig))).astype(BF16).astype(F32)
+            gc_s[:, local] = grad_conv
+            gc_all[:, here] = grad_conv[16:144]
             total = gox[16:144, here].astype(F32).reshape(16, 8, 128)
             for shift in range(8):
                 moved = gc_s[shift : shift + 152, local]
@@ -395,29 +410,13 @@
                         start = 31 - j - shift
                         total = total + tapb[j, :, here][None] * moved[start : start + 128].reshape(16, 8, 128)
             gp_s[:, local] = total.reshape(128, 128).astype(BF16)
-            gc_own = gc_s[16:144, local].reshape(16, 8, 128)
-            for shift in range(8):
-                moved = proj_s[shift : shift + 184, local]
-                for j in range(KERNEL):
-                    if (17 + j) % 8 == shift:
-                        start = 17 + j - shift
-                        partial = jnp.sum(gc_own * moved[start : start + 128].reshape(16, 8, 128), axis=0)
-                        tapg[j : j + 1, here] = jnp.sum(partial, axis=0, keepdims=True)
+        proj_all[:, at_cols(c)] = proj_s[...]
         proj_s[...] = next_s[...]
         last_s[...] = gp_s[...]
 
         @pl.when((c > 0) & (mod(c, 2) == 0))
         def _():
             rsp_copy(lax.div(c, jnp.int32(2)) - 1).start()
-
-        @pl.when(mod(c, 2) == 1)
-        def _():
-            for i in range(4):
-                peer = lax.div(c, jnp.int32(2)) * 4 + i
-
-                @pl.when(peer != me)
-                def _():
-                    ta_copy(mod(peer - me + NP, NP)).start()
 
         for at, calls in events.items():
 
@@ -425,10 +424,6 @@
             def _():
                 for call, *given in calls:
                     call(*given)
-
-        @pl.when(c == 2)
-        def _():
-            loop(0, NZ, lambda k: agp_arrived(k, 1))
 
     project(0)
     proj_s[...] = next_s[...]
@@ -440,28 +435,33 @@
 
     def ga_copy(k):
         peer = mod(f + k, FS)
-        return remote(ga_s.at[:, at128(peer)], gh.at[at128(f), :], ga_ss.at[k], ga_rs.at[k], (peer, r))
-
-    def ga_arrived(k):
-        source = mod(f - k + FS, FS)
-        remote(ga_s.at[:, at128(source)], gh.at[at128(source), :], ga_ss.at[k], ga_rs.at[k], (source, r)).wait_recv()
+        return remote(ga_s.at[:, at128(peer)], gh.at[at128(f), :], ga_ss, ga_rs, (peer, r))
 
     loop(1, FS, lambda k: ga_copy(k).start())
 
     gh[at128(f), :] = ga_s[:, at128(f)]
+    loop(0, 4, tap_grads)
+    rs(2, 0)
+    rs(1, 1)
+    rs(0, 3)
+    loop(4, 10, tap_grads)
+    rs(1, 2)
+    loop(10, NP, tap_grads)
+    rs(1, 3)
     rs(3, 0)
     rs(2, 1)
-    rs(1, 2)
-    rs(0, 3)
-    loop(1, FS, ga_arrived)
     dk_acc[...] = jnp.zeros((SPAN, HDIM), F32)
     dv_acc[...] = jnp.zeros((SPAN, HDIM), F32)
 
+    def value_back(i):
+        rows = pl.ds(pl.multiple_of(i * BLK, BLK), BLK)
+        dv_acc[...] += dot_tn(prob[rows, :], gh[rows, :])
+
     outs = ((o_gq, 0), (o_gk, 1), (o_gv, 2))
 
     def d_copy(k, ref, slot):
         peer = mod(f + k, FS)
-        return remote(dh.at[slot, at128(peer), :], ref.at[:, at128(f)], d_ss.at[slot, k], d_rs.at[slot, k], (peer, r))
+        return remote(dh.at[slot, at128(peer), :], ref.at[:, at128(f)], d_ss, d_rs.at[slot], (peer, r))
 
     def attend_back(i):
         i = mod(i + lax.div(f, jnp.int32(2)), SPAN // BLK)
@@ -481,36 +481,21 @@
                 d_copy(mod(peer - f + FS, FS), o_gq, 0).start()
 
         dk_acc[...] += dot_tn(grad_scores, qkvh[0, rows, :])
-        dv_acc[...] += dot_tn(rounded, grad)
 
     def tp_copy():
         return remote(tp_s, tp_r, tp_ss, tp_rs, partner)
 
     def tb_copy(k):
-        return remote(tb.at[z], tb.at[z], tb_ss.at[k], tb_rs.at[k], zline(mod(z + k, NZ)))
-
-    def tb_arrived(k):
-        source = mod(z - k + NZ, NZ)
-        remote(tb.at[source], tb.at[source], tb_ss.at[k], tb_rs.at[k], zline(source)).wait_recv()
+        return remote(tb.at[z], tb.at[z], tb_ss, tb_rs, zline(mod(z + k, NZ)))
 
     def tc_copy(k):
-        return remote(tc_s, tc.at[me], tc_ss.at[k], tc_rs.at[k], plane(mod(me + k, NP)))
-
-    def tc_arrived(k):
-        source = mod(me - k + NP, NP)
-        remote(tc_s, tc.at[source], tc_ss.at[k], tc_rs.at[k], plane(source)).wait_recv()
+        return remote(tc_s, tc.at[me], tc_ss, tc_rs, plane(mod(me + k, NP)))
 
     grad_scale = 1.0 / math.sqrt(SPAN * 32)
 
     def wgp_copy(half, k):
         peer = mod(me + k, NP)
-        return remote(wgp_s.at[half, peer], wgp_r.at[half, k], wgp_ss.at[half, k], wgp_rs.at[half, k], plane(peer))
-
-    def wgp_arrived(half, k):
-        source = mod(me - k + NP, NP)
-        remote(
-            wgp_s.at[half, source], wgp_r.at[half, k], wgp_ss.at[half, k], wgp_rs.at[half, k], plane(source)
-        ).wait_recv()
+        return remote(wgp_s.at[half, peer], wgp_r.at[half, k], wgp_ss, wgp_rs.at[half], plane(peer))
 
     def settle(half):
         for part in (2 * half, 2 * half + 1):
@@ -522,77 +507,68 @@
             wgp_s[half, p] = wtmp[4 * p : 4 * p + 4, half * 1024 : half * 1024 + 1024].astype(BF16)
         loop(1, NP, lambda k: wgp_copy(half, k).start())
 
-    loop(1, NP, ta_arrived)
+    all_arrived(gh.at[pl.ds(0, 896), :], ga_rs)
+    loop(0, SPAN // BLK, value_back)
+    dh[2] = dv_acc[...].astype(BF16)
+    loop(1, FS, lambda k: d_copy(k, o_gv, 2).start())
+    rs(2, 3)
+    loop(0, 1, attend_back)
+    rs(2, 2)
+    loop(1, 2, attend_back)
+    rs(3, 1)
+    loop(2, 3, attend_back)
+    rs(3, 3)
+    rs(3, 2)
+    all_arrived(ta.at[pl.ds(0, NP - 1)], ta_rs)
     total = tapg[:, at128(me)]
     for k in range(1, NP):
         total = total + ta[k]
     tp_s[...] = total
     tp_copy().start()
-    loop(0, 2, attend_back)
-    rs(3, 1)
-    rs(2, 2)
-    rs(1, 3)
+    loop(3, 4, attend_back)
     tp_copy().wait_recv()
-    tb[z] = tp_s[...] + tp_r[...]
+    tb[z] = (tp_s[...] + tp_r[...]).astype(BF16)
     loop(1, NZ, lambda k: tb_copy(k).start())
-    loop(2, 4, attend_back)
     dh[1] = (dk_acc[...] * INV_ROOT).astype(BF16)
-    dh[2] = dv_acc[...].astype(BF16)
-
-    def d_start(k):
-        d_copy(k, o_gk, 1).start()
-        d_copy(k, o_gv, 2).start()
-
-    def d_arrived(k):
-        source = mod(f - k + FS, FS)
-        for ref, slot in outs:
-            remote(
-                dh.at[slot, at128(source), :], ref.at[:, at128(source)], d_ss.at[slot, k], d_rs.at[slot, k], (source, r)
-            ).wait_recv()
-
-    loop(1, FS, d_start)
+
+    loop(1, FS, lambda k: d_copy(k, o_gk, 1).start())
     for ref, slot in outs:
         ref[:, at128(f)] = dh[slot, at128(f), :]
-    rs(3, 2)
-    rs(2, 3)
-    loop(1, NZ, tb_arrived)
-    total = tb[0]
+    settle(0)
+    settle(1)
+    all_arrived(tb.at[pl.ds(0, NZ - 1)], tb_rs)
+    total = tb[0].astype(F32)
     for k in range(1, NZ):
-        total = total + tb[k]
-    tc_s[...] = total * grad_scale
+        total = total + tb[k].astype(F32)
+    tc_s[...] = (total * grad_scale).astype(BF16)
     loop(1, NP, lambda k: tc_copy(k).start())
     tc[me] = tc_s[...]
-    settle(0)
-    rs(3, 3)
-    settle(1)
-    loop(1, NP, tc_arrived)
-    for p in range(NP):
-        o_cg[:, p * 128 : p * 128 + 128] = tc[p, 0:KERNEL, :]
-    loop(1, FS, d_arrived)
+    for ref, slot in outs:
+        all_arrived(ref.at[:, pl.ds(0, 896)], d_rs.at[slot])
     for half in range(2):
-        loop(1, NP, lambda k: wgp_arrived(half, k))
+        all_arrived(wgp_r.at[half, pl.ds(0, NP - 1)], wgp_rs.at[half])
         total = wgp_s[half, me].astype(F32)
         for k in range(1, NP):
             total = total + wgp_r[half, k].astype(F32)
         o_wg[:, half * 1024 : half * 1024 + 1024] = total * grad_scale
-
-    def plane_sent(k):
-        wpl_copy(k).wait_send()
-        ta_copy(k).wait_send()
-        tc_copy(k).wait_send()
-        for half in range(2):
-            wgp_copy(half, k).wait_send()
-
-    def span_sent(k):
-        for ref, slot in heads:
-            qkv_copy(k, ref, slot).wait_send()
-        for ref, slot in outs:
-            d_copy(k, ref, slot).wait_send()
-        att_copy(k).wait_send()
-        ga_copy(k).wait_send()
-
-    loop(1, NP, plane_sent)
-    loop(1, FS, span_sent)
+    all_arrived(tc.at[pl.ds(0, NP - 1)], tc_rs)
+    for p in range(NP):
+        o_cg[:, p * 128 : p * 128 + 128] = tc[p].astype(F32)[0:KERNEL]
+
+    all_sent(wpl.at[pl.ds(0, NP - 1)], wpl_ss)
+    all_sent(qkvh.at[:, pl.ds(0, 896), :], qkv_ss)
+    all_sent(wbuf.at[pl.ds(0, 448), :], ag_ss)
+    all_sent(wbuf.at[pl.ds(0, 512), :], agp_ss)
+    all_sent(attx.at[:, pl.ds(0, 896)], att_ss)
+    all_sent(ga_s.at[:, pl.ds(0, 896)], ga_ss)
+    all_sent(pbuf, rsp_ss)
+    all_sent(wbuf.at[pl.ds(0, 448), :], rs_ss)
+    all_sent(dh.at[:, pl.ds(0, 896), :], d_ss)
+    all_sent(wgp_s.at[:, pl.ds(0, NP - 1)], wgp_ss)
+    all_sent(ta.at[pl.ds(0, NP - 1)], ta_ss)
+    all_sent(tb.at[pl.ds(0, NZ - 1)], tb_ss)
+    all_sent(tc.at[pl.ds(0, NP - 1)], tc_ss)
+    tp_copy().wait_send()
 
     @pl.when(f > 0)
     def _():
@@ -601,20 +577,6 @@
     @pl.when(f < FS - 1)
     def _():
         go_up().wait_send()
-
-    for way in range(2):
-        for s in range(4):
-            for part in range(4):
-                if goes_far(way, s, part):
-                    ag_copy(way, s, part).wait_send()
-                if takes_part(way, s, part):
-                    rs_copy(way, s, part).wait_send()
-    for part in range(4):
-        rsp_copy(part).wait_send()
-    for pair in range(2):
-        loop(0, NZ, lambda k: agp_copy(k, pair).wait_send())
-    loop(1, NZ, lambda k: tb_copy(k).wait_send())
-    tp_copy().wait_send()
 
 
 def put_out(*refs):
@@ -665,7 +627,9 @@
             pltpu.VMEM((KERNEL, 8, D), F32),
             pltpu.VMEM((ROWS + 2 * HALO, COLS), F32),
             pltpu.VMEM((ROWS + 2 * HALO, COLS), F32),
+            pltpu.VMEM((ROWS + 2 * HALO, D), F32),
             pltpu.VMEM((160, COLS), F32),
+            pltpu.VMEM((ROWS, D), F32),
             pltpu.VMEM((ROWS, COLS), BF16),
             pltpu.VMEM((ROWS, COLS), BF16),
             pltpu.VMEM((INNER, D), BF16),
@@ -684,25 +648,25 @@
             pltpu.VMEM((NP, 32, 128), F32),
             pltpu.VMEM((32, 128), F32),
             pltpu.VMEM((32, 128), F32),
-            pltpu.VMEM((NZ, 32, 128), F32),
-            pltpu.VMEM((32, 128), F32),
-            pltpu.VMEM((NP, 32, 128), F32),
+            pltpu.VMEM((NZ, 32, 128), BF16),
+            pltpu.VMEM((32, 128), BF16),
+            pltpu.VMEM((NP, 32, 128), BF16),
             dma((6,)),
-            dma((3, FS)), dma((3, FS)),
-            dma((NP,)), dma((NP,)),
+            dma, dma((FS,)), dma((2,)),
+            dma, dma,
             dma((2,)), dma((2,)),
-            dma((2, 4, 4)), dma((2, 4, 4)),
-            dma((2, NZ)), dma((2, NZ)),
-            dma((FS,)), dma((FS,)),
-            dma((FS,)), dma((FS,)),
-            dma((4,)), dma((4,)),
-            dma((2, 4, 4)), dma((2, 4, 4)),
-            dma((3, FS)), dma((3, FS)),
-            dma((2, NP)), dma((2, NP)),
-            dma((NP,)), dma((NP,)),
+            dma, dma((2, 4, 4)),
+            dma, dma((4,)),
             dma, dma,
-            dma((NZ,)), dma((NZ,)),
-            dma((NP,)), dma((NP,)),
+            dma, dma,
+            dma, dma((4,)),
+            dma, dma((2, 4, 4)),
+            dma, dma((3,)),
+            dma, dma((2,)),
+            dma, dma,
+            dma, dma,
+            dma, dma,
+            dma, dma,
         ],
         compiler_params=pltpu.CompilerParams(
             collective_id=0, has_side_effects=True, vmem_limit_bytes=50 * 1024 * 1024

time: 102 us -> 89.7 us (0.88)
  Pallas kernels: 101 us -> 88.4 us
    pallas_call x1, Pallas kernels: 99.1 us -> 87 us  [shards(): pl.pallas_call(kernel, out_shape=shapes, in_specs=[hbm] * 6, out_specs=(v...]
where the time goes in v3:
time: 89.7 us; the launch traced here: 89 us
  Pallas kernels  88.4 us (99%)
    pallas_call x1, Pallas kernels, shards(): pl.pallas_call(kernel, out_shape=shapes, in_specs=[hbm] * 6, out_specs=(v...  87 us

profile of v3, /device:TPU:8, one launch (start us, length us, event | category | flops | bytes accessed | tf_op | source)
XLA Modules:
  0.0 89.0 jit_solution(5687722581193472802)
XLA Ops:
  0.6 87.0 %shard_map.109 = (bf16[128,2048]{1,0:T(8,128)(2,1)S(1)}, bf16[128,1024]{1,0:T(8,128)(2,1)S(1)}, bf16[128,1024]{1,0:T(8,128)(2,1)S(1)}, bf16[128,1024]{1,0:T(8,12...) custom-call(bf16[128,1024]{1,0:T(8,128)(2,1)} %bitcast.9, bf16[128,1024]{1,0:T(8,128)(2,1)} %bitcast.10, ...), custom_call_target="tpu_custom_call" | custom-call | tf_op jit(solution)/shard_map/pallas_call | solution.py:609
  87.6 1.4 %shard_map.110 = (bf16[128,2048]{1,0:T(8,128)(2,1)}, bf16[128,1024]{1,0:T(8,128)(2,1)}, bf16[128,1024]{1,0:T(8,128)(2,1)}, bf16[128,1024]{1,0:T(8,128)(2,1)}, f32[4,2048]{1,0:T(4,128)}, /*index=5*/f32[31,2048]{1,0:T(8,128)}) custom-call(bf16[128,2048]{1,0:T(8,128)(2,1)S(1)} %get-tuple-element.18.refs_0_, bf16[128,1024]{1,0:T(8,128)(2,1)S(1)} %get-tuple-element.19.refs_1_, ...), custom_call_target="tpu_custom_call" | custom-call | tf_op jit(solution)/shard_map/pallas_call | solution.py:680

commit v4 on v3

--- a/solution.py
+++ b/solution.py
@@ -65,10 +65,10 @@
     q_ref, k_ref, v_ref, w_ref, taps_ref, go_ref,
     o_block, o_gq, o_gk, o_gv, o_wg, o_cg,
     qkvh, prob, ohp, attx, wpl, wtmp, wbuf, perm, attp, attt, gox, tapv, tapb, proj_s, next_s, proj_all, gc_s, gc_all, gp_s, last_s, wgs,
-    ga_acc, ga_s, gh, dh, dk_acc, dv_acc, pbuf, sbuf, rbuf, wgp_s, wgp_r,
+    ga_acc, ga_s, gh, dh, dk_acc, dv_acc, pbuf, sbuf, rbuf, wgp_s, wgp_r, pw_s, pw_r, pz_s, pz_r,
     tapg, ta, tp_s, tp_r, tb, tc_s, tc,
     own_s, qkv_ss, q_rs, kv_rs, wpl_ss, wpl_rs, go_ss, go_rs, ag_ss, ag_rs, agp_ss, agp_rs, att_ss, att_rs,
-    ga_ss, ga_rs, rsp_ss, rsp_rs, rs_ss, rs_rs, d_ss, d_rs, wgp_ss, wgp_rs,
+    ga_ss, ga_rs, rsp_ss, rsp_rs, rs_ss, rs_rs, d_ss, d_rs, wgp_ss, wgp_rs, pw_ss, pw_rs, pz_ss, pz_rs,
     ta_ss, ta_rs, tp_ss, tp_rs, tb_ss, tb_rs, tc_ss, tc_rs,
 ):
     f = lax.axis_index("fsdp").astype(jnp.int32)
@@ -296,6 +296,7 @@
     attp[...] = jnp.dot(attx[...], perm[...], preferred_element_type=F32).astype(BF16)
     attt[...] = attp[HALO : HALO + ROWS, :].T
     agp_arrived(0)
+    grad_scale = 1.0 / math.sqrt(SPAN * 32)
     ga_acc[...] = jnp.zeros((ROWS, INNER), F32)
     tapg[KERNEL : KERNEL + 1, :] = jnp.zeros((1, D), F32)
 
@@ -346,6 +347,44 @@
             sbuf[way, s, :, cols] = value.astype(BF16)
             rs_copy(way, s, part).start()
 
+    def pw_copy(part, k):
+        peer = mod(me + k, NP)
+        return remote(pw_s.at[part, peer], pw_r.at[part, k], pw_ss, pw_rs.at[part], plane(peer))
+
+    def pz_copy(part, k):
+        other = mod(z + k, NZ)
+        return remote(pz_s.at[part, other], pz_r.at[part, k], pz_ss, pz_rs.at[part], zline(other))
+
+    def early_give(part):
+        rsp_arrived(part)
+
+        def pack(zz):
+            wtmp[:, 0:PART] = chip_sum(zz, slice(part * PART, part * PART + PART))
+            for p in range(NP):
+                pw_s[part, p, zz] = wtmp[4 * p : 4 * p + 4, 0:PART].astype(BF16)
+
+        loop(0, NZ, pack)
+        loop(1, NP, lambda k: pw_copy(part, k).start())
+
+    def early_sum(part):
+        all_arrived(pw_r.at[part, pl.ds(0, NP - 1)], pw_rs.at[part])
+
+        def add(zz):
+            total = pw_s[part, me, zz].astype(F32)
+            for k in range(1, NP):
+                total = total + pw_r[part, k, zz].astype(F32)
+            pz_s[part, zz] = total.astype(BF16)
+
+        loop(0, NZ, add)
+        loop(1, NZ, lambda k: pz_copy(part, k).start())
+
+    def early_end(part):
+        all_arrived(pz_r.at[part, pl.ds(0, NZ - 1)], pz_rs.at[part])
+        total = pz_s[part, z].astype(F32)
+        for k in range(1, NZ):
+            total = total + pz_r[part, k].astype(F32)
+        o_wg[:, part * PART : part * PART + PART] = total * grad_scale
+
     def at_cols(c):
         return pl.ds(pl.multiple_of(c * COLS, COLS), COLS)
 
@@ -360,10 +399,9 @@
     events = {
         0: ((ag_turn, 1, 3), (agp_arrived, 1)),
         2: ((ag_turn, 2, 3), (agp_arrived, 2)),
-        3: ((rs, 0, 0),),
+        3: ((early_give, 0),),
         4: ((ag_turn, 3, 3), (agp_arrived, 3)),
-        5: ((rs, 0, 1),),
-        6: ((rs, 1, 0),),
+        5: ((early_give, 1),),
         7: ((rs, 0, 2),),
     }
 
@@ -441,15 +479,14 @@
 
     gh[at128(f), :] = ga_s[:, at128(f)]
     loop(0, 4, tap_grads)
-    rs(2, 0)
-    rs(1, 1)
     rs(0, 3)
+    rs(1, 2)
     loop(4, 10, tap_grads)
-    rs(1, 2)
+    early_sum(0)
     loop(10, NP, tap_grads)
     rs(1, 3)
-    rs(3, 0)
-    rs(2, 1)
+    rs(2, 2)
+    early_sum(1)
     dk_acc[...] = jnp.zeros((SPAN, HDIM), F32)
     dv_acc[...] = jnp.zeros((SPAN, HDIM), F32)
 
@@ -491,7 +528,6 @@
     def tc_copy(k):
         return remote(tc_s, tc.at[me], tc_ss, tc_rs, plane(mod(me + k, NP)))
 
-    grad_scale = 1.0 / math.sqrt(SPAN * 32)
 
     def wgp_copy(half, k):
         peer = mod(me + k, NP)
@@ -511,13 +547,8 @@
     loop(0, SPAN // BLK, value_back)
     dh[2] = dv_acc[...].astype(BF16)
     loop(1, FS, lambda k: d_copy(k, o_gv, 2).start())
+    loop(0, 1, attend_back)
     rs(2, 3)
-    loop(0, 1, attend_back)
-    rs(2, 2)
-    loop(1, 2, attend_back)
-    rs(3, 1)
-    loop(2, 3, attend_back)
-    rs(3, 3)
     rs(3, 2)
     all_arrived(ta.at[pl.ds(0, NP - 1)], ta_rs)
     total = tapg[:, at128(me)]
@@ -525,16 +556,19 @@
         total = total + ta[k]
     tp_s[...] = total
     tp_copy().start()
-    loop(3, 4, attend_back)
+    loop(1, 2, attend_back)
     tp_copy().wait_recv()
     tb[z] = (tp_s[...] + tp_r[...]).astype(BF16)
     loop(1, NZ, lambda k: tb_copy(k).start())
+    loop(2, 4, attend_back)
     dh[1] = (dk_acc[...] * INV_ROOT).astype(BF16)
 
     loop(1, FS, lambda k: d_copy(k, o_gk, 1).start())
     for ref, slot in outs:
         ref[:, at128(f)] = dh[slot, at128(f), :]
-    settle(0)
+    rs(3, 3)
+    early_end(0)
+    early_end(1)
     settle(1)
     all_arrived(tb.at[pl.ds(0, NZ - 1)], tb_rs)
     total = tb[0].astype(F32)
@@ -545,12 +579,11 @@
     tc[me] = tc_s[...]
     for ref, slot in outs:
         all_arrived(ref.at[:, pl.ds(0, 896)], d_rs.at[slot])
-    for half in range(2):
-        all_arrived(wgp_r.at[half, pl.ds(0, NP - 1)], wgp_rs.at[half])
-        total = wgp_s[half, me].astype(F32)
-        for k in range(1, NP):
-            total = total + wgp_r[half, k].astype(F32)
-        o_wg[:, half * 1024 : half * 1024 + 1024] = total * grad_scale
+    all_arrived(wgp_r.at[1, pl.ds(0, NP - 1)], wgp_rs.at[1])
+    total = wgp_s[1, me].astype(F32)
+    for k in range(1, NP):
+        total = total + wgp_r[1, k].astype(F32)
+    o_wg[:, 1024:D] = total * grad_scale
     all_arrived(tc.at[pl.ds(0, NP - 1)], tc_rs)
     for p in range(NP):
         o_cg[:, p * 128 : p * 128 + 128] = tc[p].astype(F32)[0:KERNEL]
@@ -562,9 +595,11 @@
     all_sent(attx.at[:, pl.ds(0, 896)], att_ss)
     all_sent(ga_s.at[:, pl.ds(0, 896)], ga_ss)
     all_sent(pbuf, rsp_ss)
-    all_sent(wbuf.at[pl.ds(0, 448), :], rs_ss)
+    all_sent(wbuf.at[pl.ds(0, 224), :], rs_ss)
+    all_sent(pw_s.at[:, pl.ds(0, NP - 1)], pw_ss)
+    all_sent(pz_s.at[:, pl.ds(0, NZ - 1)], pz_ss)
     all_sent(dh.at[:, pl.ds(0, 896), :], d_ss)
-    all_sent(wgp_s.at[:, pl.ds(0, NP - 1)], wgp_ss)
+    all_sent(wgp_s.at[1, pl.ds(0, NP - 1)], wgp_ss)
     all_sent(ta.at[pl.ds(0, NP - 1)], ta_ss)
     all_sent(tb.at[pl.ds(0, NZ - 1)], tb_ss)
     all_sent(tc.at[pl.ds(0, NP - 1)], tc_ss)
@@ -644,6 +679,10 @@
             pltpu.VMEM((2, 4, 64, D), BF16),
             pltpu.VMEM((2, NP, 4, 1024), BF16),
             pltpu.VMEM((2, NP, 4, 1024), BF16),
+            pltpu.VMEM((2, NP, NZ, 4, PART), BF16),
+            pltpu.VMEM((2, NP, NZ, 4, PART), BF16),
+            pltpu.VMEM((2, NZ, 4, PART), BF16),
+            pltpu.VMEM((2, NZ, 4, PART), BF16),
             pltpu.VMEM((32, D), F32),
             pltpu.VMEM((NP, 32, 128), F32),
             pltpu.VMEM((32, 128), F32),
@@ -662,6 +701,8 @@
             dma, dma((4,)),
             dma, dma((2, 4, 4)),
             dma, dma((3,)),
+            dma, dma((2,)),
+            dma, dma((2,)),
             dma, dma((2,)),
             dma, dma,
             dma, dma,

time: 89.7 us -> 87.8 us (0.979)
  Pallas kernels: 88.4 us -> 86.5 us
    pallas_call x1, Pallas kernels: 87 us -> 85.1 us  [shards(): pl.pallas_call(kernel, out_shape=shapes, in_specs=[hbm] * 6, out_specs=(v...]
where the time goes in v4:
time: 87.8 us; the launch traced here: 87.2 us
  Pallas kernels  86.5 us (99%)
    pallas_call x1, Pallas kernels, shards(): pl.pallas_call(kernel, out_shape=shapes, in_specs=[hbm] * 6, out_specs=(v...  85.1 us

profile of v4, /device:TPU:8, one launch (start us, length us, event | category | flops | bytes accessed | tf_op | source)
XLA Modules:
  0.0 87.2 jit_solution(3537208913336776449)
XLA Ops:
  0.6 85.1 %shard_map.109 = (bf16[128,2048]{1,0:T(8,128)(2,1)S(1)}, bf16[128,1024]{1,0:T(8,128)(2,1)S(1)}, bf16[128,1024]{1,0:T(8,128)(2,1)S(1)}, bf16[128,1024]{1,0:T(8,12...) custom-call(bf16[128,1024]{1,0:T(8,128)(2,1)} %bitcast.9, bf16[128,1024]{1,0:T(8,128)(2,1)} %bitcast.10, ...), custom_call_target="tpu_custom_call" | custom-call | tf_op jit(solution)/shard_map/pallas_call | solution.py:644
  85.8 1.4 %shard_map.110 = (bf16[128,2048]{1,0:T(8,128)(2,1)}, bf16[128,1024]{1,0:T(8,128)(2,1)}, bf16[128,1024]{1,0:T(8,128)(2,1)}, bf16[128,1024]{1,0:T(8,128)(2,1)}, f32[4,2048]{1,0:T(4,128)}, /*index=5*/f32[31,2048]{1,0:T(8,128)}) custom-call(bf16[128,2048]{1,0:T(8,128)(2,1)S(1)} %get-tuple-element.18.refs_0_, bf16[128,1024]{1,0:T(8,128)(2,1)S(1)} %get-tuple-element.19.refs_1_, ...), custom_call_target="tpu_custom_call" | custom-call | tf_op jit(solution)/shard_map/pallas_call | solution.py:721

commit v5 on v4

--- a/solution.py
+++ b/solution.py
@@ -213,7 +213,7 @@
 
     ag_first(0, 1, 2)
     loop(1, FS, lambda k: qkv_copy(k, v_ref, 2).start())
-    loop(1, FS, lambda k: qkv_copy(k, q_ref, 0).start())
+    loop(1, FS, lambda k: qkv_copy(FS - k, q_ref, 0).start())
 
     @pl.when(f > 0)
     def _():
@@ -281,8 +281,7 @@
     attx[:, at128(f)] = ohp[ext(f), :]
     ag_turn(2, 0, 1, 2)
     ag_first(3)
-    ag_turn(3, 0, 1, 2)
-    ag_turn(0, 3)
+    ag_turn(3, 0)
 
     @pl.when(f < FS - 1)
     def _():
@@ -295,6 +294,7 @@
     all_arrived(attx.at[:, pl.ds(0, 896)], att_rs)
     attp[...] = jnp.dot(attx[...], perm[...], preferred_element_type=F32).astype(BF16)
     attt[...] = attp[HALO : HALO + ROWS, :].T
+    ag_turn(3, 1)
     agp_arrived(0)
     grad_scale = 1.0 / math.sqrt(SPAN * 32)
     ga_acc[...] = jnp.zeros((ROWS, INNER), F32)
@@ -397,9 +397,10 @@
         ga_acc[...] += dot_nt(gp, wbuf[:, at_cols(c)])
 
     events = {
-        0: ((ag_turn, 1, 3), (agp_arrived, 1)),
-        2: ((ag_turn, 2, 3), (agp_arrived, 2)),
-        3: ((early_give, 0),),
+        0: ((ag_turn, 3, 2), (agp_arrived, 1)),
+        1: ((ag_turn, 1, 3),),
+        2: ((agp_arrived, 2),),
+        3: ((ag_turn, 2, 3), (early_give, 0)),
         4: ((ag_turn, 3, 3), (agp_arrived, 3)),
         5: ((early_give, 1),),
         7: ((rs, 0, 2),),
@@ -464,6 +465,7 @@
                     call(*given)
 
     project(0)
+    ag_turn(0, 3)
     proj_s[...] = next_s[...]
     last_s[...] = jnp.zeros((ROWS, COLS), BF16)
     loop(0, D // COLS, columns)
@@ -569,7 +571,6 @@
     rs(3, 3)
     early_end(0)
     early_end(1)
-    settle(1)
     all_arrived(tb.at[pl.ds(0, NZ - 1)], tb_rs)
     total = tb[0].astype(F32)
     for k in range(1, NZ):
@@ -577,6 +578,7 @@
     tc_s[...] = (total * grad_scale).astype(BF16)
     loop(1, NP, lambda k: tc_copy(k).start())
     tc[me] = tc_s[...]
+    settle(1)
     for ref, slot in outs:
         all_arrived(ref.at[:, pl.ds(0, 896)], d_rs.at[slot])
     all_arrived(wgp_r.at[1, pl.ds(0, NP - 1)], wgp_rs.at[1])
@@ -615,16 +617,12 @@
 
 
 def put_out(*refs):
-    sources, targets, rooms, into, out = refs[:6], refs[6:12], refs[12:18], refs[18], refs[19]
-    loads = [pltpu.make_async_copy(sources[i], rooms[i], into.at[i]) for i in range(6)]
-    stores = [pltpu.make_async_copy(rooms[i], targets[i], out.at[i]) for i in range(6)]
-    for load in loads:
-        load.start()
-    for load, store in zip(loads, stores):
-        load.wait()
-        store.start()
-    for store in stores:
-        store.wait()
+    sources, targets, sems = refs[:6], refs[6:12], refs[12]
+    copies = [pltpu.make_async_copy(sources[i], targets[i], sems.at[i]) for i in range(6)]
+    for copy in copies:
+        copy.start()
+    for copy in copies:
+        copy.wait()
 
 
 def shards(queries, key_rows, value_rows, out_weight, conv_weight, grad_out):
@@ -723,7 +721,7 @@
         out_shape=shapes,
         in_specs=[anywhere] * 6,
         out_specs=(hbm,) * 6,
-        scratch_shapes=[pltpu.VMEM(*result) for result in results] + [dma((6,)), dma((6,))],
+        scratch_shapes=[dma((6,))],
         compiler_params=pltpu.CompilerParams(vmem_limit_bytes=8 * 1024 * 1024),
     )(*found)
     return (block_out[None], grad_queries[None], grad_keys[None], grad_values[None], weight_grad, conv_grad)

time: 87.8 us -> 84.7 us (0.965)
  Pallas kernels: 86.5 us -> 83.8 us
    pallas_call x1, Pallas kernels: 85.1 us -> 82.6 us  [shards(): pl.pallas_call(kernel, out_shape=shapes, in_specs=[hbm] * 6, out_specs=(v...]
where the time goes in v5:
time: 84.7 us; the launch traced here: 84.4 us
  Pallas kernels  83.8 us (99%)
    pallas_call x1, Pallas kernels, shards(): pl.pallas_call(kernel, out_shape=shapes, in_specs=[hbm] * 6, out_specs=(v...  82.6 us

profile of v5, /device:TPU:8, one launch (start us, length us, event | category | flops | bytes accessed | tf_op | source)
XLA Modules:
  0.0 84.4 jit_solution(10612572379043549224)
XLA Ops:
  0.6 82.6 %shard_map.109 = (bf16[128,2048]{1,0:T(8,128)(2,1)S(1)}, bf16[128,1024]{1,0:T(8,128)(2,1)S(1)}, bf16[128,1024]{1,0:T(8,128)(2,1)S(1)}, bf16[128,1024]{1,0:T(8,12...) custom-call(bf16[128,1024]{1,0:T(8,128)(2,1)} %bitcast.9, bf16[128,1024]{1,0:T(8,128)(2,1)} %bitcast.10, ...), custom_call_target="tpu_custom_call" | custom-call | tf_op jit(solution)/shard_map/pallas_call | solution.py:642
  83.2 1.2 %shard_map.110 = (bf16[128,2048]{1,0:T(8,128)(2,1)}, bf16[128,1024]{1,0:T(8,128)(2,1)}, bf16[128,1024]{1,0:T(8,128)(2,1)}, bf16[128,1024]{1,0:T(8,128)(2,1)}, f32[4,2048]{1,0:T(4,128)}, /*index=5*/f32[31,2048]{1,0:T(8,128)}) custom-call(bf16[128,2048]{1,0:T(8,128)(2,1)S(1)} %get-tuple-element.18.refs_0_, bf16[128,1024]{1,0:T(8,128)(2,1)S(1)} %get-tuple-element.19.refs_1_, ...), custom_call_target="tpu_custom_call" | custom-call | tf_op jit(solution)/shard_map/pallas_call | solution.py:719

commit v6 on v5

--- a/solution.py
+++ b/solution.py
@@ -401,8 +401,7 @@
         1: ((ag_turn, 1, 3),),
         2: ((agp_arrived, 2),),
         3: ((ag_turn, 2, 3), (early_give, 0)),
-        4: ((ag_turn, 3, 3), (agp_arrived, 3)),
-        5: ((early_give, 1),),
+        4: ((ag_turn, 3, 3), (agp_arrived, 3), (early_give, 1)),
         7: ((rs, 0, 2),),
     }
 

time: 84.7 us -> 83.9 us (level)
  no operation moved by 1% of the time
where the time goes in v6:
time: 83.9 us; the launch traced here: 83.7 us
  Pallas kernels  83.1 us (99%)
    pallas_call x1, Pallas kernels, shards(): pl.pallas_call(kernel, out_shape=shapes, in_specs=[hbm] * 6, out_specs=(v...  81.9 us

profile of v6, /device:TPU:8, one launch (start us, length us, event | category | flops | bytes accessed | tf_op | source)
XLA Modules:
  0.0 83.7 jit_solution(5750607950498305647)
XLA Ops:
  0.6 81.9 %shard_map.109 = (bf16[128,2048]{1,0:T(8,128)(2,1)S(1)}, bf16[128,1024]{1,0:T(8,128)(2,1)S(1)}, bf16[128,1024]{1,0:T(8,128)(2,1)S(1)}, bf16[128,1024]{1,0:T(8,12...) custom-call(bf16[128,1024]{1,0:T(8,128)(2,1)} %bitcast.9, bf16[128,1024]{1,0:T(8,128)(2,1)} %bitcast.10, ...), custom_call_target="tpu_custom_call" | custom-call | tf_op jit(solution)/shard_map/pallas_call | solution.py:641
  82.5 1.2 %shard_map.110 = (bf16[128,2048]{1,0:T(8,128)(2,1)}, bf16[128,1024]{1,0:T(8,128)(2,1)}, bf16[128,1024]{1,0:T(8,128)(2,1)}, bf16[128,1024]{1,0:T(8,128)(2,1)}, f32[4,2048]{1,0:T(4,128)}, /*index=5*/f32[31,2048]{1,0:T(8,128)}) custom-call(bf16[128,2048]{1,0:T(8,128)(2,1)S(1)} %get-tuple-element.18.refs_0_, bf16[128,1024]{1,0:T(8,128)(2,1)S(1)} %get-tuple-element.19.refs_1_, ...), custom_call_target="tpu_custom_call" | custom-call | tf_op jit(solution)/shard_map/pallas_call | solution.py:718
